TPU v7x, 32 devices: a whole 2x2x4 slice. The times are simulated.
32 devices in a mesh: ctx: 2 (over x), tp: 4 (over z), fsdp: 4 (over y, core).
Axes of the slice: x: 2, y: 2, z: 4, core: 2. Of those that a mesh axis runs over, the one named last changes fastest.
Arguments:
- x_in: bfloat16 [2, 4, 1024, 2048], P(None, 'fsdp', 'ctx', 'tp'), may hold values from -6 to 6
- cotangent: bfloat16 [2, 4, 1024, 2048], P(None, 'fsdp', 'ctx', 'tp'), may hold values from -6 to 6
- offsets: int32 [2, 4, 4], P(None, 'fsdp'), may hold values from 0 to 960, as said below
- in_gain: float32 [2048], replicated, may hold values from 0.1 to 1.9
- w_z: bfloat16 [2048, 4096], P('fsdp', 'tp'), may hold values from -0.125 to 0.125
- w_x: bfloat16 [2048, 4096], P('fsdp', 'tp'), may hold values from -0.125 to 0.125
- w_dt: bfloat16 [2048, 64], P('fsdp', 'tp'), may hold values from -0.125 to 0.125
- w_bc: bfloat16 [2048, 256], P('fsdp', 'tp'), may hold values from -0.125 to 0.125
- conv_w: float32 [4, 4352], replicated, may hold values from -3 to 3
- conv_b: float32 [4352], replicated, may hold values from -0.5 to 0.5
- dt_bias: float32 [64], replicated, may hold values from -3 to -1
- a_log: float32 [64], replicated, may hold values from -9 to -1
- d_skip: float32 [64], replicated, may hold values from 0.5 to 1.5
- norm_gain: float32 [4096], replicated, may hold values from 0.1 to 1.9
- w_out: bfloat16 [4096, 2048], P('tp', 'fsdp'), may hold values from -0.09375 to 0.09375
Outputs:
- out: float32 [2, 4, 1024, 2048], P(None, 'fsdp', 'ctx', 'tp')
- d_x_in: float32 [2, 4, 1024, 2048], P(None, 'fsdp', 'ctx', 'tp')
- g_in_gain: float32 [2048], replicated
- g_w_z: float32 [2048, 4096], P(('ctx', 'fsdp'), 'tp')
- g_w_x: float32 [2048, 4096], P(('ctx', 'fsdp'), 'tp')
- g_w_dt: float32 [2048, 64], P(('ctx', 'fsdp'), 'tp')
- g_w_bc: float32 [2048, 256], P(('ctx', 'fsdp'), 'tp')
- g_conv_w: float32 [4, 4352], replicated
- g_conv_b: float32 [4352], replicated
- g_dt_bias: float32 [64], replicated
- g_a_log: float32 [64], replicated
- g_d_skip: float32 [64], replicated
- g_norm_gain: float32 [4096], replicated
- g_w_out: float32 [4096, 2048], P('tp', ('ctx', 'fsdp'))
Inputs may be any that keep to these rules, and one draw needn't show every extreme that they name: Each row of offsets starts at 0 and rises strictly; one document of every sequence begins within its first 512 positions and ends within its last 512; the last document of every sequence begins at 1024 - 512 // (2 * 4).
All inputs are finite; a program needn't handle non-finite values.
Results may differ from a plain program's by a relative error of at most 0.011.
Values may be sent and summed in bfloat16 or wider, within the bound.
A program may use at most 256 MiB of HBM per device.

v0:
```python
import jax
import jax.numpy as jnp
from jax import lax
from jax.sharding import PartitionSpec as P

STRETCH = 256


EPSILON = 1e-05
PRECISE = lax.Precision.HIGHEST


def passed_along(shard, axis, by):
    peers = lax.axis_size(axis)
    pairs = [(i, i + by) for i in range(peers) if 0 <= i + by < peers]
    return lax.ppermute(shard, axis, pairs)


def prefix(shard, axis, combine, identity, reverse):
    peers, place = (lax.axis_size(axis), lax.axis_index(axis))
    everything = jax.tree.map(lambda part: lax.all_gather(part, axis), shard)
    start = jax.tree.map(
        lambda part, zero: jnp.broadcast_to(jnp.asarray(zero, part.dtype), part.shape),
        shard,
        identity,
    )

    def step(k, before):
        at = peers - 1 - k if reverse else k
        reached = at > place if reverse else at < place
        new = combine(before, jax.tree.map(lambda part: part[at], everything))
        return jax.tree.map(lambda a, b: jnp.where(reached, a, b), new, before)

    return lax.fori_loop(0, peers, step, start)


def exact_dot(first_op, second_op):
    return jnp.dot(first_op, second_op, precision=PRECISE, preferred_element_type=jnp.float32)


def plain_dot(first_op, second_op):
    return jnp.dot(first_op, second_op, preferred_element_type=jnp.float32)


def rows_dot(first_op, second_op, precision=None):
    return lax.dot_general(
        first_op,
        second_op,
        (((0,), (0,)), ((), ())),
        precision=precision,
        preferred_element_type=jnp.float32,
    )


def cols_dot(first_op, second_op, precision=None):
    return lax.dot_general(
        first_op,
        second_op,
        (((1,), (1,)), ((), ())),
        precision=precision,
        preferred_element_type=jnp.float32,
    )


def silu_slope(pre_act):
    sig_val = jax.nn.sigmoid(pre_act)
    return sig_val * (1.0 + pre_act * (1.0 - sig_val))


def doc_numbers(starts, places):
    return jnp.sum((starts[..., None, :] <= places[..., :, None]).astype(jnp.int32), axis=-1) - 1


def stretch_step(carry_state, inputs):
    values, write_vec, read_vec, log_decay, step_size, doc_ids, before = inputs
    span_len = doc_ids.shape[0]
    running = jnp.cumsum(log_decay, axis=0)
    places = jnp.arange(span_len)
    same_doc = (doc_ids[:, None] == doc_ids[None, :]) & (places[:, None] >= places[None, :])
    scores = exact_dot(read_vec, write_vec.T)
    by_head = running.T
    spread_log = by_head[:, :, None] - by_head[:, None, :]
    allowed = same_doc[None, :, :]
    weights = jnp.where(allowed, jnp.exp(jnp.where(allowed, spread_log, 0.0)), 0.0)
    weights = weights * scores[None, :, :] * step_size.T[:, None, :]
    result = jnp.einsum("hts,shp->thp", weights, values, precision=PRECISE)
    kept_mask = (doc_ids == before).astype(jnp.float32)
    lead_decay = jnp.exp(running) * kept_mask[:, None]
    result = result + lead_decay[:, :, None] * jnp.einsum(
        "tn,hpn->thp", read_vec, carry_state, precision=PRECISE
    )
    tail_decay = (
        jnp.exp(running[-1][None, :] - running)
        * (doc_ids == doc_ids[-1]).astype(jnp.float32)[:, None]
        * step_size
    )
    fresh_state = jnp.einsum(
        "shp,sn->hpn", tail_decay[:, :, None] * values, write_vec, precision=PRECISE
    )
    return (lead_decay[-1][:, None, None] * carry_state + fresh_state, result)


def local_scan(values, write_vec, read_vec, log_decay, step_size, doc_ids):
    length = doc_ids.shape[0]
    blocks = length // STRETCH
    before = jnp.concatenate(
        [jnp.full((1,), -1, jnp.int32), doc_ids[STRETCH - 1 : length - 1 : STRETCH]]
    )

    def blocked(tensor):
        return tensor.reshape((blocks, STRETCH) + tensor.shape[1:])

    start_state = jnp.zeros((values.shape[1], values.shape[2], write_vec.shape[1]), jnp.float32)
    final_state, results = lax.scan(
        jax.checkpoint(stretch_step),
        start_state,
        (
            blocked(values),
            blocked(write_vec),
            blocked(read_vec),
            blocked(log_decay),
            blocked(step_size),
            blocked(doc_ids),
            before,
        ),
    )
    return (results.reshape(values.shape), final_state)


def chain(earlier, later):
    return (earlier[0] * later[0], later[0][..., None, None] * earlier[1] + later[1])


def embed(segment, full_len, offset, axis_pos):
    full_shape = list(segment.shape)
    full_shape[axis_pos] = full_len
    return lax.dynamic_update_slice_in_dim(
        jnp.zeros(full_shape, jnp.float32), segment, offset, axis_pos
    )


def add_pairs(first_set, second_set):
    return tuple((left_item + right_item for left_item, right_item in zip(first_set, second_set)))


def on_device(
    x_in,
    cotangent,
    offsets,
    in_gain,
    w_z,
    w_x,
    w_dt,
    w_bc,
    conv_w,
    conv_b,
    dt_bias,
    a_log,
    d_skip,
    norm_gain,
    w_out,
):
    batches, seq_count, length, width_dev = x_in.shape
    tokens = seq_count * length
    tp_rank = lax.axis_index("tp")
    ctx_rank = lax.axis_index("ctx")
    inner_dev = w_z.shape[1]
    heads_dev = w_dt.shape[1]
    head_width = inner_dev // heads_dev
    model_width = in_gain.shape[0]
    inner_width = norm_gain.shape[0]
    head_count = dt_bias.shape[0]
    state_pair = conv_w.shape[1] - inner_width
    state_width = state_pair // 2
    kernel_len = conv_w.shape[0]
    rim_len = kernel_len - 1
    chan_w = jnp.concatenate(
        [
            lax.dynamic_slice_in_dim(conv_w, tp_rank * inner_dev, inner_dev, 1),
            conv_w[:, inner_width:],
        ],
        axis=1,
    )
    chan_b = jnp.concatenate(
        [lax.dynamic_slice_in_dim(conv_b, tp_rank * inner_dev, inner_dev, 0), conv_b[inner_width:]]
    )
    gate_gain = lax.dynamic_slice_in_dim(norm_gain, tp_rank * inner_dev, inner_dev, 0)
    local_gain = lax.dynamic_slice_in_dim(in_gain, tp_rank * width_dev, width_dev, 0)
    bias_dev = lax.dynamic_slice_in_dim(dt_bias, tp_rank * heads_dev, heads_dev, 0)
    decay_rate = -jnp.exp(lax.dynamic_slice_in_dim(a_log, tp_rank * heads_dev, heads_dev, 0))
    skip_dev = lax.dynamic_slice_in_dim(d_skip, tp_rank * heads_dev, heads_dev, 0)
    first_pos = ctx_rank * length
    places = first_pos + jnp.arange(length, dtype=jnp.int32)
    rim_places = first_pos - rim_len + jnp.arange(length + rim_len, dtype=jnp.int32)
    out_rows = []
    grad_rows = []
    big_sums = None
    small_sums = None
    for batch_idx in range(batches):
        full_z, full_xw, full_dt, rows_bc, full_out = (
            lax.all_gather(w_z, "fsdp", axis=0, tiled=True),
            lax.all_gather(w_x, "fsdp", axis=0, tiled=True),
            lax.all_gather(w_dt, "fsdp", axis=0, tiled=True),
            lax.all_gather(w_bc, "fsdp", axis=0, tiled=True),
            lax.all_gather(w_out, "fsdp", axis=1, tiled=True),
        )
        starts = offsets[batch_idx]
        doc_ids = doc_numbers(starts, places)
        doc_rim = doc_numbers(starts, rim_places)
        before_dev = doc_numbers(starts, places[:1] - 1)
        kept_mask = (doc_ids == before_dev).astype(jnp.float32)
        flat_in = x_in[batch_idx].reshape(tokens, width_dev)
        full_in, full_bc = (
            lax.all_gather(flat_in, "tp", axis=1, tiled=True),
            lax.all_gather(rows_bc, "tp", axis=1, tiled=True),
        )
        resid = full_in.astype(jnp.float32)
        inv_rms = lax.rsqrt(jnp.mean(resid * resid, axis=1, keepdims=True) + EPSILON)
        normed = (resid * inv_rms * in_gain).astype(jnp.bfloat16)
        gate_raw = plain_dot(normed, full_z)
        conv_x = plain_dot(normed, full_xw).astype(jnp.bfloat16)
        conv_bc = plain_dot(normed, full_bc).astype(jnp.bfloat16)
        step_pre = plain_dot(normed, full_dt).reshape(seq_count, length, heads_dev) + bias_dev
        conv_in = jnp.concatenate([conv_x, conv_bc], axis=1).reshape(
            seq_count, length, inner_dev + state_pair
        )
        rim_rows = passed_along(conv_in[:, length - rim_len :], "ctx", 1)
        extended = jnp.concatenate([rim_rows, conv_in], axis=1).astype(jnp.float32)
        matches = [
            (doc_rim[:, k : k + length] == doc_ids).astype(jnp.float32)[..., None]
            for k in range(kernel_len)
        ]
        conv_out = jnp.broadcast_to(chan_b, (seq_count, length, inner_dev + state_pair))
        for k in range(kernel_len):
            conv_out = conv_out + chan_w[k] * extended[:, k : k + length] * matches[k]
        activ = jax.nn.silu(conv_out)
        values = activ[..., :inner_dev].reshape(seq_count, length, heads_dev, head_width)
        write_vec = activ[..., inner_dev : inner_dev + state_width]
        read_vec = activ[..., inner_dev + state_width :]
        step_size = jax.nn.softplus(step_pre)
        log_decay = step_size * decay_rate

        def local_part(values_in, write_in, read_in, decay_in, step_in):
            return jax.vmap(local_scan)(values_in, write_in, read_in, decay_in, step_in, doc_ids)

        (core_out, local_state), local_pull = jax.vjp(
            local_part, values, write_vec, read_vec, log_decay, step_size
        )

        def lead_of(decay_in):
            return jnp.exp(jnp.cumsum(decay_in, axis=1)) * kept_mask[..., None]

        lead_decay, lead_pull = jax.vjp(lead_of, log_decay)
        decay_dev = lead_decay[:, -1]
        state_in = prefix(
            (decay_dev, local_state),
            "ctx",
            chain,
            (jnp.ones_like(decay_dev), jnp.zeros_like(local_state)),
            False,
        )[1]
        carried = jnp.einsum("sln,shpn->slhp", read_vec, state_in, precision=PRECISE)
        mixed = core_out + lead_decay[..., None] * carried + skip_dev[:, None] * values
        mixed_flat = mixed.reshape(tokens, inner_dev)
        gate_act = jax.nn.silu(gate_raw)
        gated = mixed_flat * gate_act
        square_sum = lax.psum(jnp.sum(gated * gated, axis=1), "tp")
        gate_rms = lax.rsqrt(square_sum[:, None] / inner_width + EPSILON)
        gate_norm = (gated * gate_rms * gate_gain).astype(jnp.bfloat16)
        partial_out = plain_dot(gate_norm, full_out)
        out_share = lax.psum_scatter(partial_out, "tp", scatter_dimension=1, tiled=True)
        resid_dev = flat_in.astype(jnp.float32)
        out_rows.append((resid_dev + out_share).reshape(seq_count, length, width_dev))
        flat_back = cotangent[batch_idx].reshape(tokens, width_dev)
        full_back = lax.all_gather(flat_back, "tp", axis=1, tiled=True)
        grad_out = rows_dot(gate_norm, full_back)
        d_norm = cols_dot(full_back, full_out)
        g_gate_gain = jnp.sum(d_norm * gated * gate_rms, axis=0)
        scaled = d_norm * gate_gain
        gate_dot = lax.psum(jnp.sum(scaled * gated, axis=1), "tp")
        d_gated = gate_rms * scaled - gated * gate_rms**3 * gate_dot[:, None] / inner_width
        d_core = (d_gated * gate_act).reshape(seq_count, length, heads_dev, head_width)
        d_gate = (d_gated * mixed_flat * silu_slope(gate_raw)).astype(jnp.bfloat16)
        g_skip = jnp.sum(d_core * values, axis=(0, 1, 3))
        weighted = lead_decay[..., None] * d_core
        g_state = jnp.einsum("slhp,sln->shpn", weighted, read_vec, precision=PRECISE)
        d_state = prefix(
            (decay_dev, g_state),
            "ctx",
            chain,
            (jnp.ones_like(decay_dev), jnp.zeros_like(g_state)),
            True,
        )[1]
        d_lead = jnp.sum(d_core * carried, axis=3)
        d_lead = d_lead.at[:, -1].add(jnp.sum(d_state * state_in, axis=(2, 3)))
        d_read_carry = jnp.einsum("slhp,shpn->sln", weighted, state_in, precision=PRECISE)
        d_values, d_write, d_read, d_decay, d_step = local_pull((d_core, d_state))
        d_decay = d_decay + lead_pull(d_lead)[0]
        d_values = d_values + skip_dev[:, None] * d_core
        d_read = d_read + d_read_carry
        g_rate = jnp.sum(d_decay * step_size, axis=(0, 1)) * decay_rate
        d_pre = (d_step + d_decay * decay_rate) * jax.nn.sigmoid(step_pre)
        g_bias = jnp.sum(d_pre, axis=(0, 1))
        d_activ = jnp.concatenate(
            [d_values.reshape(seq_count, length, inner_dev), d_write, d_read], axis=2
        )
        d_conv = d_activ * silu_slope(conv_out)
        g_chan_b = jnp.sum(d_conv, axis=(0, 1))
        d_extended = jnp.zeros_like(extended)
        tap_grads = []
        for k in range(kernel_len):
            masked = d_conv * matches[k]
            tap_grads.append(jnp.sum(masked * extended[:, k : k + length], axis=(0, 1)))
            d_extended = d_extended + jnp.pad(
                chan_w[k] * masked, ((0, 0), (k, rim_len - k), (0, 0))
            )
        g_chan_w = jnp.stack(tap_grads)
        back_rim = passed_along(d_extended[:, :rim_len], "ctx", -1)
        d_conv_in = d_extended[:, rim_len:] + jnp.pad(
            back_rim, ((0, 0), (length - rim_len, 0), (0, 0))
        )
        d_conv_x = d_conv_in[..., :inner_dev].reshape(tokens, inner_dev).astype(jnp.bfloat16)
        d_conv_bc = d_conv_in[..., inner_dev:].reshape(tokens, state_pair)
        d_step_low = d_pre.reshape(tokens, heads_dev).astype(jnp.bfloat16)
        d_normed = (
            cols_dot(d_gate, full_z)
            + cols_dot(d_conv_x, full_xw)
            + cols_dot(d_step_low, full_dt)
            + cols_dot(d_conv_bc, full_bc.astype(jnp.float32), PRECISE)
        )
        grad_z = rows_dot(normed, d_gate)
        grad_x = rows_dot(normed, d_conv_x)
        grad_dt = rows_dot(normed, d_step_low)
        normed_share, bc_share = (
            lax.psum_scatter(d_normed, "tp", scatter_dimension=1, tiled=True),
            lax.psum_scatter(d_conv_bc, "tp", scatter_dimension=1, tiled=True),
        )
        grad_bc = rows_dot(normed.astype(jnp.float32), bc_share, PRECISE)
        scaled_in = normed_share * local_gain
        in_dot = lax.psum(jnp.sum(scaled_in * resid_dev, axis=1), "tp")
        g_in_dev = jnp.sum(normed_share * resid_dev * inv_rms, axis=0)
        d_resid = (
            flat_back.astype(jnp.float32)
            + inv_rms * scaled_in
            - resid_dev * inv_rms**3 * in_dot[:, None] / model_width
        )
        grad_rows.append(d_resid.reshape(seq_count, length, width_dev))
        small_now = (
            embed(g_in_dev, model_width, tp_rank * width_dev, 0),
            jnp.concatenate(
                [
                    embed(g_chan_w[:, :inner_dev], inner_width, tp_rank * inner_dev, 1),
                    g_chan_w[:, inner_dev:],
                ],
                axis=1,
            ),
            jnp.concatenate(
                [
                    embed(g_chan_b[:inner_dev], inner_width, tp_rank * inner_dev, 0),
                    g_chan_b[inner_dev:],
                ]
            ),
            embed(g_bias, head_count, tp_rank * heads_dev, 0),
            embed(g_rate, head_count, tp_rank * heads_dev, 0),
            embed(g_skip, head_count, tp_rank * heads_dev, 0),
            embed(g_gate_gain, inner_width, tp_rank * inner_dev, 0),
        )
        small_sums = small_now if small_sums is None else add_pairs(small_sums, small_now)
        big_now = (grad_z, grad_x, grad_dt, grad_bc, grad_out)
        reduced = (
            lax.psum_scatter(big_now[0], ("ctx", "fsdp"), scatter_dimension=0, tiled=True),
            lax.psum_scatter(big_now[1], ("ctx", "fsdp"), scatter_dimension=0, tiled=True),
            lax.psum_scatter(big_now[2], ("ctx", "fsdp"), scatter_dimension=0, tiled=True),
            lax.psum_scatter(big_now[3], ("ctx", "fsdp"), scatter_dimension=0, tiled=True),
            lax.psum_scatter(big_now[4], ("ctx", "fsdp"), scatter_dimension=1, tiled=True),
        )
        big_sums = reduced if big_sums is None else add_pairs(big_sums, reduced)
    small_total = lax.psum(
        (
            small_sums[0],
            small_sums[1],
            small_sums[2],
            small_sums[3],
            small_sums[4],
            small_sums[5],
            small_sums[6],
        ),
        ("ctx", "tp", "fsdp"),
    )
    return (
        jnp.stack(out_rows),
        jnp.stack(grad_rows),
        small_total[0],
        big_sums[0],
        big_sums[1],
        big_sums[2],
        big_sums[3],
        small_total[1],
        small_total[2],
        small_total[3],
        small_total[4],
        small_total[5],
        small_total[6],
        big_sums[4],
    )


def solution(mesh):
    in_specs = (
        P(None, "fsdp", "ctx", "tp"),
        P(None, "fsdp", "ctx", "tp"),
        P(None, "fsdp", None),
        P(),
        P("fsdp", "tp"),
        P("fsdp", "tp"),
        P("fsdp", "tp"),
        P("fsdp", "tp"),
        P(),
        P(),
        P(),
        P(),
        P(),
        P(),
        P("tp", "fsdp"),
    )
    out_specs = (
        P(None, "fsdp", "ctx", "tp"),
        P(None, "fsdp", "ctx", "tp"),
        P(),
        P(("ctx", "fsdp"), "tp"),
        P(("ctx", "fsdp"), "tp"),
        P(("ctx", "fsdp"), "tp"),
        P(("ctx", "fsdp"), "tp"),
        P(),
        P(),
        P(),
        P(),
        P(),
        P(),
        P("tp", ("ctx", "fsdp")),
    )
    return jax.shard_map(
        on_device, mesh=mesh, in_specs=in_specs, out_specs=out_specs, check_vma=False
    )
```

profile of v0, /device:TPU:0, one launch (start us, length us, event | category | flops | bytes accessed | tf_op | source)
XLA Modules:
  0.0 1655.2 jit_solution(12467761942024263608)
XLA Ops:
  10.4 7.7 all_gather.71
  35.4 23.5 %all-gather.33.cloned.1.call-done = bf16[1,1,512,2048]{3,2,1,0:T(8,128)(2,1)} async-done(((bf16[1,1,512,512]{3,2,1,0:T(8,128)(2,1)}), bf16[1,1,512,2048]{3,2,1,0:T(8,128)(2,1)}) %all-gather.33.cloned.1.call-update) | async-done | bytes 2097168 | tf_op jit(solution)/shard_map/all_gather | solution.py:214
  65.1 40.6 %all-gather.29.cloned.1.call-done = bf16[1,1,512,2048]{3,2,1,0:T(8,128)(2,1)} async-done(((bf16[1,1,512,512]{3,2,1,0:T(8,128)(2,1)}), bf16[1,1,512,2048]{3,2,1,0:T(8,128)(2,1)}) %all-gather.29.cloned.1.call-update) | async-done | bytes 2097168 | tf_op jit(solution)/shard_map/all_gather | solution.py:214
  111.6 22.3 %all-gather.23.cloned.1.call-done = bf16[2048,256]{0,1:T(8,128)(2,1)} async-done(((bf16[2048,64]{0,1:T(8,128)(2,1)}), bf16[2048,256]{0,1:T(8,128)(2,1)}) %all-gather.23.cloned.1.call-update) | async-done | bytes 1048592 | tf_op jit(solution)/shard_map/all_gather | solution.py:215
  138.9 30.5 %all-gather.21.cloned.1.call-done = bf16[2048,1024]{1,0:T(8,128)(2,1)} async-done(((bf16[512,1024]{1,0:T(8,128)(2,1)}), bf16[2048,1024]{1,0:T(8,128)(2,1)}) %all-gather.21.cloned.1.call-update) | async-done | bytes 4194320 | tf_op jit(solution)/shard_map/all_gather | solution.py:202
  216.2 86.1 %while.148 = (s32[]{:T(128)}, f32[1,16,64,128]{3,2,1,0:T(8,128)S(1)}, f32[2,1,256,16,64]{2,0,4,3,1:T(2,128)}, f32[2,1,16,64,128]{4,3,2,1,0:T(8,128)}, f32[2,1,25...) while((s32[]{:T(128)}, ...), condition=%wide.region_21.22_spmd.clone, body=%wide.region_18.21_spmd.clone.sunk | while | flops 1718703104 | bytes 30595968 | solution.py:114
  233.8 21.9 %dynamic_update_slice.243 = f32[2,1,256,16,64]{2,0,4,3,1:T(2,128)} dynamic-update-slice(f32[2,1,256,16,64]{2,0,4,3,1:T(2,128)} %get-tuple-element.3018, f32[1,1,256,16,64]{2,0,4,3,1:T(1,128)S(1)} %copy.838, s32[]{:T(128)} %get-tuple-element.3016, s32[]{:T(128)} %constant.418.clone.1..sunk.4, s32[]{:T(128)} %constant.418.clone.1..sunk.4, s32[]{:T(128)} %constant.418.clone.1..sunk.4, ...) | dynamic-update-slice | bytes 2097156 | tf_op jit(solution)/shard_map/jvp(vmap())/while/body/jit(dynamic_update_index_in_dim)/dynamic_update_slice | solution.py:114
  276.6 21.9 %dynamic_update_slice.243 = f32[2,1,256,16,64]{2,0,4,3,1:T(2,128)} dynamic-update-slice(f32[2,1,256,16,64]{2,0,4,3,1:T(2,128)} %get-tuple-element.3018, f32[1,1,256,16,64]{2,0,4,3,1:T(1,128)S(1)} %copy.838, s32[]{:T(128)} %get-tuple-element.3016, s32[]{:T(128)} %constant.418.clone.1..sunk.4, s32[]{:T(128)} %constant.418.clone.1..sunk.4, s32[]{:T(128)} %constant.418.clone.1..sunk.4, ...) | dynamic-update-slice | bytes 2097156 | tf_op jit(solution)/shard_map/jvp(vmap())/while/body/jit(dynamic_update_index_in_dim)/dynamic_update_slice | solution.py:114
  306.4 83.2 %while.146 = (s32[]{:T(128)}, f32[1,16,64,128]{3,2,1,0:T(8,128)S(1)}, f32[2,1,256,16,64]{2,0,4,3,1:T(2,128)}, f32[2,1,16,64,128]{4,3,2,1,0:T(8,128)}, f32[2,1,25...) while((s32[]{:T(128)}, ...), condition=%wide.region_6.7_spmd.clone, body=%wide.region_3.6_spmd.clone.sunk | while | flops 1718703104 | bytes 23247656 | solution.py:114
  315.6 6.2 fusion.559
  322.9 21.9 %dynamic_update_slice.241 = f32[2,1,256,16,64]{2,0,4,3,1:T(2,128)} dynamic-update-slice(f32[2,1,256,16,64]{2,0,4,3,1:T(2,128)} %get-tuple-element.2976, f32[1,1,256,16,64]{2,0,4,3,1:T(1,128)S(1)} %copy.828, s32[]{:T(128)} %get-tuple-element.2974, s32[]{:T(128)} %constant.418.clone.1..sunk.2, s32[]{:T(128)} %constant.418.clone.1..sunk.2, s32[]{:T(128)} %constant.418.clone.1..sunk.2, ...) | dynamic-update-slice | bytes 2097156 | tf_op jit(solution)/shard_map/jvp(vmap())/while/body/jit(dynamic_update_index_in_dim)/dynamic_update_slice | solution.py:114
  357.0 6.2 fusion.559
  364.3 21.9 %dynamic_update_slice.241 = f32[2,1,256,16,64]{2,0,4,3,1:T(2,128)} dynamic-update-slice(f32[2,1,256,16,64]{2,0,4,3,1:T(2,128)} %get-tuple-element.2976, f32[1,1,256,16,64]{2,0,4,3,1:T(1,128)S(1)} %copy.828, s32[]{:T(128)} %get-tuple-element.2974, s32[]{:T(128)} %constant.418.clone.1..sunk.2, s32[]{:T(128)} %constant.418.clone.1..sunk.2, s32[]{:T(128)} %constant.418.clone.1..sunk.2, ...) | dynamic-update-slice | bytes 2097156 | tf_op jit(solution)/shard_map/jvp(vmap())/while/body/jit(dynamic_update_index_in_dim)/dynamic_update_slice | solution.py:114
  411.7 6.7 fusion.243
  433.3 8.2 multiply_add_fusion.3
  447.8 7.6 multiply_reduce_fusion.23
  459.4 11.7 all-reduce.17
  471.1 23.6 %all-gather.37.cloned.1.call-done = bf16[1,1,512,2048]{3,2,1,0:T(8,128)(2,1)} async-done(((bf16[1,1,512,512]{3,2,1,0:T(8,128)(2,1)}), bf16[1,1,512,2048]{3,2,1,0:T(8,128)(2,1)}) %all-gather.37.cloned.1.call-update) | async-done | bytes 2097168 | tf_op jit(solution)/shard_map/all_gather | solution.py:275
  494.7 8.8 multiply_reduce_fusion.17
  503.5 9.4 all-reduce.16
  512.9 10.7 fusion.241
  574.7 6.5 fusion.358
  585.8 8.8 all-gather.39.cloned.1.call-done
  602.1 88.7 %while.145 = (s32[]{:T(128)}, f32[1,16,64,128]{3,2,1,0:T(8,128)S(1)}, f32[2,1,256,16,64]{2,4,3,1,0:T(8,128)}, f32[2,1,256,128]{3,2,0,1:T(8,128)}, f32[2,1,256,12...) while((s32[]{:T(128)}, ...), condition=%wide.region_72.73_spmd, body=%wide.region_59.72_spmd.sunk | while | flops 3951035392 | bytes 37898104 | solution.py:114
  609.4 7.7 fusion.539
  635.8 6.0 fusion.542
  653.5 7.7 fusion.539
  679.9 6.0 fusion.542
  704.8 87.7 %while.144 = (s32[]{:T(128)}, f32[1,16,64,128]{3,2,1,0:T(8,128)S(1)}, f32[2,1,256,16,64]{2,4,3,1,0:T(8,128)}, f32[2,1,256,128]{3,2,0,1:T(8,128)}, f32[2,1,256,12...) while((s32[]{:T(128)}, ...), condition=%wide.region_47.48_spmd, body=%wide.region_34.47_spmd.sunk | while | flops 3951035392 | bytes 36063096 | solution.py:114
  712.9 7.7 fusion.512
  738.7 6.0 fusion.515
  756.6 7.7 fusion.512
  887.3 6.6 fusion.335
  895.5 6.5 fusion.334
  902.2 8.4 fusion.245
  921.1 10.4 convolution_add_fusion.2
  954.7 24.1 %reduce-scatter.22.cloned.1.call-done = f32[512,512]{1,0:T(8,128)} async-done(((f32[512,2048]{1,0:T(8,128)}), f32[512,512]{1,0:T(8,128)}) %reduce-scatter.22.cloned.1.call-update) | async-done | bytes 1048592 | tf_op jit(solution)/shard_map/reduce_scatter | solution.py:335
  978.8 79.5 %reduce-scatter.20.cloned.1.call-done = f32[512,512]{1,0:T(8,128)} async-done(((f32[512,2048]{1,0:T(8,128)}), f32[512,512]{1,0:T(8,128)}) %reduce-scatter.20.cloned.1.call-update) | async-done | bytes 1048592 | tf_op jit(solution)/shard_map/reduce_scatter | solution.py:335
  1061.0 11.0 all-reduce.15
  1072.2 43.6 %all-reduce.14 = (f32[2048]{0:T(1024)}, f32[4352]{0:T(1024)}, f32[64]{0:T(128)}, f32[64]{0:T(128)}, f32[64]{0:T(128)}, /*index=5*/f32[4096]{0:T(1024)}) all-reduce(f32[2048]{0:T(1024)S(1)} %add_dynamic-update-slice_fusion.1, f32[4352]{0:T(1024)S(1)} %maximum_add_fusion, ...), channel_id=1, replica_groups=mesh['ctx'=2,'tp'=4,'fsdp'=4] {'ctx','tp','fsdp'}, use_global_device_ids=true, to_apply=%region_82.83 | all-reduce | flops 10688 | bytes 85504 | tf_op jit(solution)/shard_map/psum | solution.py:378
  1115.9 23.1 %reduce-scatter.18.cloned.1.call-done = f32[512,512]{1,0:T(8,128)} async-done(((f32[512,2048]{1,0:T(8,128)}), f32[512,512]{1,0:T(8,128)}) %reduce-scatter.18.cloned.1.call-update) | async-done | bytes 1048592 | tf_op jit(solution)/shard_map/reduce_scatter | solution.py:271
  1139.0 79.5 %reduce-scatter.16.cloned.1.call-done = f32[512,512]{1,0:T(8,128)} async-done(((f32[512,2048]{1,0:T(8,128)}), f32[512,512]{1,0:T(8,128)}) %reduce-scatter.16.cloned.1.call-update) | async-done | bytes 1048592 | tf_op jit(solution)/shard_map/reduce_scatter | solution.py:271
  1223.7 119.2 %all-reduce.20.cloned.1.call-done = f32[4,4352]{1,0:T(4,128)} async-done(((f32[4,4352]{1,0:T(4,128)}), f32[4,4352]{1,0:T(4,128)}) %all-reduce.20.cloned.1.call-update) | async-done | bytes 69648 | tf_op jit(solution)/shard_map/psum | solution.py:378
  1343.0 39.1 %reduce-scatter.28.cloned.1.call-done = f32[256,16]{0,1:T(8,128)} async-done(((f32[2048,16]{0,1:T(8,128)}), f32[256,16]{0,1:T(8,128)}) %reduce-scatter.28.cloned.1.call-update) | async-done | bytes 16400 | tf_op jit(solution)/shard_map/reduce_scatter | solution.py:373
  1382.0 38.2 %reduce-scatter.30.cloned.1.call-done = f32[256,64]{0,1:T(8,128)} async-done(((f32[2048,64]{0,1:T(8,128)}), f32[256,64]{0,1:T(8,128)}) %reduce-scatter.30.cloned.1.call-update) | async-done | bytes 65552 | tf_op jit(solution)/shard_map/reduce_scatter | solution.py:374
  1420.2 75.3 %reduce-scatter.32.cloned.1.call-done = f32[1024,256]{1,0:T(8,128)} async-done(((f32[1024,2048]{1,0:T(8,128)}), f32[1024,256]{1,0:T(8,128)}) %reduce-scatter.32.cloned.1.call-update) | async-done | bytes 1048592 | tf_op jit(solution)/shard_map/reduce_scatter | solution.py:375
  1495.5 75.7 %reduce-scatter.24.cloned.1.call-done = f32[256,1024]{1,0:T(8,128)} async-done(((f32[2048,1024]{1,0:T(8,128)}), f32[256,1024]{1,0:T(8,128)}) %reduce-scatter.24.cloned.1.call-update) | async-done | bytes 1048592 | tf_op jit(solution)/shard_map/reduce_scatter | solution.py:371
  1571.2 75.2 %reduce-scatter.26.cloned.1.call-done = f32[256,1024]{1,0:T(8,128)} async-done(((f32[2048,1024]{1,0:T(8,128)}), f32[256,1024]{1,0:T(8,128)}) %reduce-scatter.26.cloned.1.call-update) | async-done | bytes 1048592 | tf_op jit(solution)/shard_map/reduce_scatter | solution.py:372
  (1139 shorter events, 551.2 us)
Async XLA Ops:
  7.2 51.7 %all-gather.33.cloned.1.call-start = ((), (), s32[]{:S(2)}) async-start(), calls=%async_computation.22 | async-start | bytes 2621440 | tf_op jit(solution)/shard_map/all_gather | solution.py:214
  9.6 96.1 %all-gather.29.cloned.1.call-start = ((), (), s32[]{:S(2)}) async-start(), calls=%async_computation.20 | async-start | bytes 2621440 | tf_op jit(solution)/shard_map/all_gather | solution.py:214
  10.4 123.6 %all-gather.23.cloned.1.call-start = ((), (), s32[]{:S(2)}) async-start(), calls=%async_computation.12 | async-start | bytes 1310720 | tf_op jit(solution)/shard_map/all_gather | solution.py:215
  18.2 151.2 %all-gather.21.cloned.1.call-start = ((), (), s32[]{:S(2)}) async-start(), calls=%async_computation.11 | async-start | bytes 5242880 | tf_op jit(solution)/shard_map/all_gather | solution.py:202
  18.8 392.9 %all-gather.41.cloned.1.call-start = ((), (), s32[]{:S(2)}) async-start(), calls=%async_computation.26 | async-start | bytes 2621440 | tf_op jit(solution)/shard_map/all_gather | solution.py:275
  20.0 391.7 %all-gather.27.cloned.1.call-start = ((), (), s32[]{:S(2)}) async-start(), calls=%async_computation.14 | async-start | bytes 5242880 | tf_op jit(solution)/shard_map/all_gather | solution.py:205
  20.5 404.6 %all-gather.35.cloned.1.call-start = ((), (), s32[]{:S(2)}) async-start(), calls=%async_computation.23 | async-start | bytes 1572864 | tf_op jit(solution)/shard_map/all_gather | solution.py:21
  25.3 157.4 %copy-start.153 = (f32[1,512]{1,0:T(1,128)}, f32[1,512]{1,0:T(1,128)S(1)}, u32[]{:S(2)}) copy-start(f32[1,512]{1,0:T(1,128)S(1)} %get-tuple-element.2316) | copy-start | bytes 6148
  25.3 157.4 %copy-start.155 = (f32[1,512]{1,0:T(1,128)}, f32[1,512]{1,0:T(1,128)S(1)}, u32[]{:S(2)}) copy-start(f32[1,512]{1,0:T(1,128)S(1)} %get-tuple-element.2317) | copy-start | bytes 6148
  25.3 157.4 %copy-start.157 = (f32[1,512]{1,0:T(1,128)}, f32[1,512]{1,0:T(1,128)S(1)}, u32[]{:S(2)}) copy-start(f32[1,512]{1,0:T(1,128)S(1)} %get-tuple-element.2318) | copy-start | bytes 6148
  25.3 157.4 %copy-start.159 = (f32[1,512]{1,0:T(1,128)}, f32[1,512]{1,0:T(1,128)S(1)}, u32[]{:S(2)}) copy-start(f32[1,512]{1,0:T(1,128)S(1)} %get-tuple-element.2319) | copy-start | bytes 6148
  33.2 155.9 %copy-start.161 = (f32[1,512]{1,0:T(1,128)}, f32[1,512]{1,0:T(1,128)S(1)}, u32[]{:S(2)}) copy-start(f32[1,512]{1,0:T(1,128)S(1)} %get-tuple-element.2312) | copy-start | bytes 6148
  33.2 155.9 %copy-start.163 = (f32[1,512]{1,0:T(1,128)}, f32[1,512]{1,0:T(1,128)S(1)}, u32[]{:S(2)}) copy-start(f32[1,512]{1,0:T(1,128)S(1)} %get-tuple-element.2313) | copy-start | bytes 6148
  33.3 155.9 %copy-start.165 = (f32[1,512]{1,0:T(1,128)}, f32[1,512]{1,0:T(1,128)S(1)}, u32[]{:S(2)}) copy-start(f32[1,512]{1,0:T(1,128)S(1)} %get-tuple-element.2314) | copy-start | bytes 6148
  33.3 155.9 %copy-start.167 = (f32[1,512]{1,0:T(1,128)}, f32[1,512]{1,0:T(1,128)S(1)}, u32[]{:S(2)}) copy-start(f32[1,512]{1,0:T(1,128)S(1)} %get-tuple-element.2315) | copy-start | bytes 6148
  33.4 155.8 %copy-start.121 = (f32[1280]{0:T(1024)}, f32[1280]{0:T(1024)S(1)}, u32[]{:S(2)}) copy-start(f32[1280]{0:T(1024)S(1)} %get-tuple-element.2046) | copy-start | bytes 15364
  33.4 155.8 %copy-start.123 = (f32[1280]{0:T(1024)}, f32[1280]{0:T(1024)S(1)}, u32[]{:S(2)}) copy-start(f32[1280]{0:T(1024)S(1)} %get-tuple-element.2047) | copy-start | bytes 15364
  33.4 155.8 %copy-start.125 = (f32[1280]{0:T(1024)}, f32[1280]{0:T(1024)S(1)}, u32[]{:S(2)}) copy-start(f32[1280]{0:T(1024)S(1)} %get-tuple-element.2048) | copy-start | bytes 15364
  33.4 155.8 %copy-start.127 = (f32[1280]{0:T(1024)}, f32[1280]{0:T(1024)S(1)}, u32[]{:S(2)}) copy-start(f32[1280]{0:T(1024)S(1)} %get-tuple-element.2049) | copy-start | bytes 15364
  61.5 107.8 %copy-start.142 = (f32[512]{0:T(512)}, f32[512]{0:T(512)S(1)}, u32[]{:S(2)}) copy-start(f32[512]{0:T(512)S(1)} %get-tuple-element.2330) | copy-start | bytes 6148
  174.9 7.6 collective-permute-start.1
  180.9 8.0 collective-permute-start
  303.1 124.5 %all-gather.31.cloned.1.call-start = ((), (), s32[]{:S(2)}) async-start(), calls=%async_computation.21 | async-start | bytes 1572864 | tf_op jit(solution)/shard_map/all_gather | solution.py:21
  390.4 57.3 %all-gather.25.cloned.1.call-start = ((), (), s32[]{:S(2)}) async-start(), calls=%async_computation.13 | async-start | bytes 5242880 | tf_op jit(solution)/shard_map/all_gather | solution.py:201
  391.2 103.5 %all-gather.37.cloned.1.call-start = ((), (), s32[]{:S(2)}) async-start(), calls=%async_computation.24 | async-start | bytes 2621440 | tf_op jit(solution)/shard_map/all_gather | solution.py:275
  391.8 190.8 %all-gather.43.cloned.1.call-start = ((), (), s32[]{:S(2)}) async-start(), calls=%async_computation.27 | async-start | bytes 1572864 | tf_op jit(solution)/shard_map/all_gather | solution.py:21
  393.9 119.0 %copy-start.100 = (f32[1024]{0:T(1024)}, f32[1024]{0:T(1024)S(1)}, u32[]{:S(2)}) copy-start(f32[1024]{0:T(1024)S(1)} %dynamic_slice.346) | copy-start | bytes 12292
  533.8 60.8 %all-gather.39.cloned.1.call-start = ((), (), s32[]{:S(2)}) async-start(), calls=%async_computation.25 | async-start | bytes 1572864 | tf_op jit(solution)/shard_map/all_gather | solution.py:21
  574.6 340.4 %reduce-scatter.34.cloned.1.call-start = ((), (), s32[]{:S(2)}) async-start(), calls=%async_computation.33 | async-start | bytes 655360
  827.2 32.0 %collective-permute-start.3 = (f32[1,3,1280]{2,1,0:T(4,128)S(1)}, f32[1,3,1280]{2,1,0:T(4,128)S(1)}, u32[]{:S(2)}, u32[]{:S(2)}) collective-permute-start(f32[1,3,1280]{2,1,0:T(4,128)S(1)} %pad_add_fusion.2), channel_id=1, source_target_pairs={{16,0},{17,1},{18,2},{19,3},{20,4},{21,5},{22,6},{23,7},{24,8},{25... | collective-permute-start | bytes 46088 | tf_op jit(solution)/shard_map/ppermute | solution.py:16
  830.3 22.0 %collective-permute-start.2 = (f32[1,3,1280]{2,1,0:T(4,128)S(1)}, f32[1,3,1280]{2,1,0:T(4,128)S(1)}, u32[]{:S(2)}, u32[]{:S(2)}) collective-permute-start(f32[1,3,1280]{2,1,0:T(4,128)S(1)} %pad_add_fusion.3), channel_id=1, source_target_pairs={{16,0},{17,1},{18,2},{19,3},{20,4},{21,5},{22,6},{23,7},{24,8},{25... | collective-permute-start | bytes 46088 | tf_op jit(solution)/shard_map/ppermute | solution.py:16
  855.1 62.0 %reduce-scatter.36.cloned.1.call-start = ((), (), s32[]{:S(2)}) async-start(), calls=%async_computation.34 | async-start | bytes 655360
  860.7 118.1 %reduce-scatter.22.cloned.1.call-start = ((), (), s32[]{:S(2)}) async-start(), calls=%async_computation.18 | async-start | bytes 5242880 | tf_op jit(solution)/shard_map/reduce_scatter | solution.py:335
  871.0 187.4 %reduce-scatter.20.cloned.1.call-start = ((), (), s32[]{:S(2)}) async-start(), calls=%async_computation.17 | async-start | bytes 5242880 | tf_op jit(solution)/shard_map/reduce_scatter | solution.py:335
  885.7 253.2 %reduce-scatter.18.cloned.1.call-start = ((), (), s32[]{:S(2)}) async-start(), calls=%async_computation.16 | async-start | bytes 5242880 | tf_op jit(solution)/shard_map/reduce_scatter | solution.py:271
  894.0 324.4 %reduce-scatter.16.cloned.1.call-start = ((), (), s32[]{:S(2)}) async-start(), calls=%async_computation.15 | async-start | bytes 5242880 | tf_op jit(solution)/shard_map/reduce_scatter | solution.py:271
  902.1 440.8 %all-reduce.20.cloned.1.call-start = ((), (), s32[]{:S(2)}) async-start(), calls=%async_computation.19 | async-start | bytes 139264 | tf_op jit(solution)/shard_map/psum | solution.py:378
  911.9 470.1 %reduce-scatter.28.cloned.1.call-start = ((), (), s32[]{:S(2)}) async-start(), calls=%async_computation.30 | async-start | bytes 147456 | tf_op jit(solution)/shard_map/reduce_scatter | solution.py:373
  914.9 505.3 %reduce-scatter.30.cloned.1.call-start = ((), (), s32[]{:S(2)}) async-start(), calls=%async_computation.31 | async-start | bytes 589824 | tf_op jit(solution)/shard_map/reduce_scatter | solution.py:374
  921.0 574.5 %reduce-scatter.32.cloned.1.call-start = ((), (), s32[]{:S(2)}) async-start(), calls=%async_computation.32 | async-start | bytes 9437184 | tf_op jit(solution)/shard_map/reduce_scatter | solution.py:375
  931.5 639.7 %reduce-scatter.24.cloned.1.call-start = ((), (), s32[]{:S(2)}) async-start(), calls=%async_computation.28 | async-start | bytes 9437184 | tf_op jit(solution)/shard_map/reduce_scatter | solution.py:371
  941.6 704.9 %reduce-scatter.26.cloned.1.call-start = ((), (), s32[]{:S(2)}) async-start(), calls=%async_computation.29 | async-start | bytes 9437184 | tf_op jit(solution)/shard_map/reduce_scatter | solution.py:372
  951.8 106.5 %copy-start.62 = (bf16[2,1,512,512]{3,2,1,0:T(8,128)(2,1)S(1)}, bf16[2,1,512,512]{3,2,1,0:T(8,128)(2,1)}, u32[]{:S(2)}) copy-start(bf16[2,1,512,512]{3,2,1,0:T(8,128)(2,1)} %param.35) | copy-start | bytes 3145732
  951.9 106.5 %copy-start.152 = (f32[512]{0:T(512)S(1)}, f32[512]{0:T(512)}, u32[]{:S(2)}) copy-start(f32[512]{0:T(512)} %copy-done.151) | copy-start | bytes 6148
  951.9 266.5 %copy-start.78 = (bf16[2,1,512,512]{3,2,1,0:T(8,128)(2,1)S(1)}, bf16[2,1,512,512]{3,2,1,0:T(8,128)(2,1)}, u32[]{:S(2)}) copy-start(bf16[2,1,512,512]{3,2,1,0:T(8,128)(2,1)} %param.36) | copy-start | bytes 3145732
  951.9 266.5 %copy-start.182 = (f32[512]{0:T(512)S(1)}, f32[512]{0:T(512)}, u32[]{:S(2)}) copy-start(f32[512]{0:T(512)} %get-tuple-element.2329) | copy-start | bytes 6148
  951.9 266.5 %copy-start.183 = (f32[512]{0:T(512)S(1)}, f32[512]{0:T(512)}, u32[]{:S(2)}) copy-start(f32[512]{0:T(512)} %get-tuple-element.2327) | copy-start | bytes 6148
  978.8 239.6 %copy-start.79 = (f32[512,512]{1,0:T(8,128)S(1)}, f32[512,512]{1,0:T(8,128)}, u32[]{:S(2)}) copy-start(f32[512,512]{1,0:T(8,128)} %reduce-scatter.22.cloned.1.call-done) | copy-start | bytes 3145732
  (216 other events, 2066.8 us)
Sparse Core Ops, SparseCore 0:
  10.2 48.6 all-gather.32
  61.0 44.6 all-gather.28
  107.3 26.6 all-gather.22
  135.4 33.9 all-gather.20
  170.8 45.9 all-gather.40
  218.2 33.1 all-gather.26
  303.2 20.3 all-gather.34
  390.6 20.3 all-gather.30
  412.5 34.5 all-gather.24
  448.5 46.1 all-gather.36
  533.9 19.8 all-gather.42
  574.7 19.8 all-gather.38
  855.3 23.7 reduce-scatter.33
  881.7 19.8 reduce-scatter.35
  903.8 74.9 reduce-scatter.21
  981.1 77.2 reduce-scatter.19
  1060.5 78.4 reduce-scatter.17
  1141.2 77.1 reduce-scatter.15
  1224.6 118.3 all-reduce.19
  1346.4 35.5 reduce-scatter.27
  1386.0 34.1 reduce-scatter.29
  1424.2 71.2 reduce-scatter.31
  1499.9 71.2 reduce-scatter.23
  1575.1 71.2 reduce-scatter.25
where the time goes:
time: 1670 us; the launch traced here: 1660 us
  waiting for transfers between devices  782 us (47%)
  local copies, waits for them, and re-layouts  303 us (18%)
  matrix products  303 us (18%)
  other arithmetic  137 us (8%)
  blocking collectives  97 us (6%)
  between operations  19.4 us (1%)
    psum x1, waiting for transfers between devices, on_device(): lax.psum((small_sums[0], small_sums[1], small_sums[2], small_sums[3], sma...  119 us
    reduce_scatter x2, waiting for transfers between devices, on_device(): lax.psum_scatter(d_normed, 'tp', scatter_dimension=1, tiled=True)  104 us
    reduce_scatter x2, waiting for transfers between devices, on_device(): lax.psum_scatter(partial_out, 'tp', scatter_dimension=1, tiled=True)  103 us
    dynamic_update_slice x24, local copies, waits for them, and re-layouts, local_scan(): lax.scan(jax.checkpoint(stretch_step), start_state, (blocked(values), blo...  99.8 us
    dot_general x12, matrix products, stretch_step(): result = jnp.einsum('hts,shp->thp', weights, values, precision=PRECISE)  77.1 us
    reduce_scatter x1, waiting for transfers between devices, on_device(): lax.psum_scatter(big_now[0], ('ctx', 'fsdp'), scatter_dimension=0, tiled=...  75.7 us
    reduce_scatter x1, waiting for transfers between devices, on_device(): lax.psum_scatter(big_now[4], ('ctx', 'fsdp'), scatter_dimension=1, tiled=...  75.3 us
    reduce_scatter x1, waiting for transfers between devices, on_device(): lax.psum_scatter(big_now[1], ('ctx', 'fsdp'), scatter_dimension=0, tiled=...  75.2 us
  transfers between devices with their start and end apart: 28, of which 16 were waited for; matrix products, arithmetic and copies ran while one was open for 28% of the time, Pallas kernels for 0%

commit v1 on v0

v1 whole, which is shorter than its diff:
```python
import functools

import jax
import jax.numpy as jnp
from jax import lax
from jax.experimental import pallas as pl
from jax.experimental.pallas import tpu as pltpu
from jax.sharding import PartitionSpec as P

EPSILON = 1e-05
PRECISE = lax.Precision.HIGHEST
LANES = 128
CHUNK = 128
FAR = -1e30
F32 = jnp.float32
BF16 = jnp.bfloat16


def mm(a, b, dims=((1,), (0,)), precision=None):
    return lax.dot_general(a, b, (dims, ((), ())), precision=precision, preferred_element_type=F32)


NN = ((1,), (0,))
NT = ((1,), (1,))
TN = ((0,), (0,))


def softplus(v):
    return jnp.maximum(v, 0.0) + jnp.log1p(jnp.exp(-jnp.abs(v)))


def silu_slope(v, sig):
    return sig * (1.0 + v * (1.0 - sig))


def doc_of(off_ref, seq, pos):
    count = jnp.zeros_like(pos)
    for j in range(off_ref.shape[1]):
        count = count + (off_ref[seq, j] <= pos).astype(jnp.int32)
    return count


def widen(cols, head, lane, width):
    out = cols[:, head : head + 1]
    for i in range(1, LANES // width):
        out = jnp.where(lane >= i * width, cols[:, head + i : head + i + 1], out)
    return jnp.broadcast_to(out, (cols.shape[0], LANES))


class Span:
    def __init__(self, off_ref, pos_ref, seq, start, q, dtr, dtb, rate, taps):
        first = pos_ref[0]
        at = first + start
        col = at + lax.broadcasted_iota(jnp.int32, (q, 1), 0)
        row = at + lax.broadcasted_iota(jnp.int32, (1, q), 1)
        dcol = doc_of(off_ref, seq, col)
        drow = doc_of(off_ref, seq, row)
        before = doc_of(off_ref, seq, at - 1)
        before_dev = doc_of(off_ref, seq, first - 1)
        last = doc_of(off_ref, seq, at + q - 1)
        self.match = [
            (doc_of(off_ref, seq, col - (taps - 1 - k)) == dcol).astype(F32) for k in range(taps - 1)
        ]
        self.far = jnp.where((dcol == drow) & (col >= row), 0.0, FAR)
        self.kept = (dcol == before).astype(F32)
        self.kept_dev = (dcol == before_dev).astype(F32)
        self.carry_dev = (before == before_dev).astype(F32)
        self.dt_in = dtr + dtb
        self.dt = softplus(self.dt_in)
        decay = self.dt * rate
        tri = (
            lax.broadcasted_iota(jnp.int32, (q, q), 0) >= lax.broadcasted_iota(jnp.int32, (q, q), 1)
        ).astype(F32)
        self.tri = tri
        self.cum = mm(tri, decay, precision=PRECISE)
        self.cum_t = self.cum.T
        self.lead = jnp.exp(self.cum) * self.kept
        end = self.cum[q - 1 : q, :]
        self.tail = jnp.exp(end - self.cum) * (dcol == last).astype(F32)
        self.end = end

    def fade(self, head):
        return jnp.exp(self.cum[:, head : head + 1] - self.cum_t[head : head + 1, :] + self.far)


def conv_block(pre, halo, cw, cb, match):
    taps = len(match) + 1
    ext = jnp.concatenate([halo, pre], axis=0)
    shifted = [
        pltpu.roll(ext, taps - 1 - k, 0)[8:] * match[k] for k in range(taps - 1)
    ] + [pre]
    conv = cb
    for k in range(taps):
        conv = conv + cw[k : k + 1] * shifted[k]
    return conv, shifted


def scan_kernel(dims, off, pos, pre, rim, dtr, cw, cb, dtb, rate, dsk, y, rd, lead, st, lead0, fin, halo, state, run):
    q, inner, width, n = dims
    b, c = pl.program_id(0), pl.program_id(1)

    @pl.when(c == 0)
    def _():
        halo[...] = rim[0]
        state[...] = jnp.zeros_like(state)
        run[...] = jnp.zeros_like(run)

    taps = cw.shape[0]
    sp = Span(off, pos, b, c * q, q, dtr[0], dtb[...], rate[...], taps)
    total = run[...] + sp.cum
    lead[0] = jnp.exp(total) * sp.kept_dev
    lead0[0, 0] = jnp.broadcast_to(jnp.exp(run[...]) * sp.carry_dev, (8, LANES))
    run[...] = total[q - 1 : q]

    def act(lo, hi):
        conv, _ = conv_block(
            pre[0, :, lo:hi].astype(F32), halo[:, lo:hi], cw[:, lo:hi], cb[:, lo:hi], sp.match
        )
        return conv * jax.nn.sigmoid(conv)

    write = act(inner, inner + n).astype(BF16)
    read = act(inner + n, inner + 2 * n).astype(BF16)
    rd[0] = read
    scores = mm(read, write, NT)
    write_t = write.astype(F32).T.astype(BF16)
    lane = lax.broadcasted_iota(jnp.int32, (1, LANES), 1)
    per = LANES // width
    for j in range(inner // LANES):
        lo, hi = j * LANES, (j + 1) * LANES
        h = j * per
        xs = act(lo, hi)
        xdt = xs * widen(sp.dt, h, lane, width)
        xdt_low = xdt.astype(BF16)
        mixed = None
        for i in range(per):
            part = mm((sp.fade(h + i) * scores).astype(BF16), xdt_low)
            mixed = part if mixed is None else jnp.where(lane >= i * width, part, mixed)
        old = state[:, lo:hi]
        st[0, 0, :, lo:hi] = old
        mixed = mixed + widen(sp.lead, h, lane, width) * mm(read, old.astype(BF16))
        y[0, :, lo:hi] = mixed + dsk[:, lo:hi] * xs
        fresh = mm(write_t, (xdt * widen(sp.tail, h, lane, width)).astype(BF16))
        new = widen(sp.lead[q - 1 : q], h, lane, width) * old + fresh
        state[:, lo:hi] = new
        fin[0, :, lo:hi] = new
    halo[...] = pre[0, q - 8 : q].astype(F32)


def gate_kernel(dims, y_in, rd, lead, lead0, st, s_in, z, gain, y, ygg, sq, st_full):
    q, inner, width, n = dims
    lane = lax.broadcasted_iota(jnp.int32, (1, LANES), 1)
    per = LANES // width
    total = jnp.zeros((q, LANES), F32)
    for j in range(inner // LANES):
        lo, hi = j * LANES, (j + 1) * LANES
        h = j * per
        came = s_in[0, :, lo:hi]
        st_full[0, 0, :, lo:hi] = st[0, 0, :, lo:hi] + widen(lead0[0, 0, 0:1], h, lane, width) * came
        val = y_in[0, :, lo:hi] + widen(lead[0], h, lane, width) * mm(rd[0], came.astype(BF16))
        y[0, :, lo:hi] = val
        gate = z[0, :, lo:hi]
        gated = val * gate * jax.nn.sigmoid(gate)
        total = total + gated * gated
        ygg[0, :, lo:hi] = (gated * gain[:, lo:hi]).astype(BF16)
    sq[0] = jnp.broadcast_to(jnp.sum(total, axis=1, keepdims=True), (q, LANES))


def ungate_kernel(dims, count, dyn, y, z, stat, gain, rd, lead, dy, dz, yn, g_gain, g_state):
    q, inner, width, n = dims
    b, c = pl.program_id(0), pl.program_id(1)

    @pl.when((b == 0) & (c == 0))
    def _():
        g_gain[...] = jnp.zeros_like(g_gain)

    @pl.when(c == 0)
    def _():
        g_state[...] = jnp.zeros_like(g_state)

    lane = lax.broadcasted_iota(jnp.int32, (1, LANES), 1)
    per = LANES // width
    r2 = stat[0, :, 0:1]
    coef = r2 * r2 * r2 * stat[0, :, 1:2] * (1.0 / count)
    read_t = rd[0].astype(F32).T.astype(BF16)
    for j in range(inner // LANES):
        lo, hi = j * LANES, (j + 1) * LANES
        h = j * per
        gate = z[0, :, lo:hi]
        sig = jax.nn.sigmoid(gate)
        act = gate * sig
        val = y[0, :, lo:hi]
        gated = val * act
        dn = dyn[0, :, lo:hi]
        g = gain[:, lo:hi]
        norm = gated * r2
        g_gain[0:1, lo:hi] += jnp.sum(dn * norm, axis=0, keepdims=True)
        yn[0, :, lo:hi] = (norm * g).astype(BF16)
        d_gated = r2 * (dn * g) - gated * coef
        d_core = d_gated * act
        dy[0, :, lo:hi] = d_core
        dz[0, :, lo:hi] = (d_gated * val * silu_slope(gate, sig)).astype(BF16)
        g_state[0, :, lo:hi] += mm(read_t, (d_core * widen(lead[0], h, lane, width)).astype(BF16))


def back_kernel(dims, off, pos, pre, prev, rim, dtr, y, dy, st, d_in, cw, cb, dtb, rate, dsk,
                dcat, ddt_out, edge, rim_grad, acc, acc_head, d_state, carry):
    q, inner, width, n = dims
    b, c = pl.program_id(0), pl.program_id(1)
    chunks = pl.num_programs(1)
    at = chunks - 1 - c

    @pl.when((b == 0) & (c == 0))
    def _():
        acc[...] = jnp.zeros_like(acc)
        acc_head[...] = jnp.zeros_like(acc_head)

    @pl.when(c == 0)
    def _():
        d_state[...] = d_in[0]
        carry[...] = jnp.zeros_like(carry)

    taps = cw.shape[0]
    sp = Span(off, pos, b, at * q, q, dtr[0], dtb[...], rate[...], taps)
    lane = lax.broadcasted_iota(jnp.int32, (1, LANES), 1)
    per = LANES // width

    def conv(lo, hi):
        ahead = jnp.where(at == 0, rim[0, :, lo:hi], prev[0, 8:16, lo:hi].astype(F32))
        return conv_block(pre[0, :, lo:hi].astype(F32), ahead, cw[:, lo:hi], cb[:, lo:hi], sp.match)

    def unconv(lo, hi, d_act, out, shifted, sig):
        d_conv = d_act * silu_slope(out, sig)
        acc[taps : taps + 1, lo:hi] += jnp.sum(d_conv, axis=0, keepdims=True)
        d_ext = None
        zeros = jnp.zeros((8, hi - lo), F32)
        for k in range(taps):
            acc[k : k + 1, lo:hi] += jnp.sum(d_conv * shifted[k], axis=0, keepdims=True)
            masked = cw[k : k + 1, lo:hi] * d_conv
            if k < taps - 1:
                masked = masked * sp.match[k]
            part = jnp.concatenate([zeros, masked], axis=0)
            if k < taps - 1:
                part = pltpu.roll(part, q + 8 - (taps - 1 - k), 0)
            d_ext = part if d_ext is None else d_ext + part
        d_pre = jnp.concatenate([d_ext[8:q], d_ext[q:] + carry[:, lo:hi]], axis=0)
        carry[:, lo:hi] = d_ext[0:8]
        rim_grad[0, :, lo:hi] = d_ext[0:8]
        dcat[0, :, lo:hi] = d_pre.astype(BF16)

        @pl.when(c == 0)
        def _():
            edge[0, :, lo:hi] = d_pre[q - 8 : q]

    w_conv, w_shift = conv(inner, inner + n)
    w_sig = jax.nn.sigmoid(w_conv)
    write = (w_conv * w_sig).astype(BF16)
    r_conv, r_shift = conv(inner + n, inner + 2 * n)
    r_sig = jax.nn.sigmoid(r_conv)
    read = (r_conv * r_sig).astype(BF16)
    scores = mm(read, write, NT)
    read_t = read.astype(F32).T.astype(BF16)
    d_scores = jnp.zeros((q, q), F32)
    d_write = jnp.zeros((q, n), F32)
    d_read = jnp.zeros((q, n), F32)
    d_cum = jnp.zeros((q, LANES), F32)
    d_step = jnp.zeros((q, LANES), F32)
    d_end = jnp.zeros((8, LANES), F32)
    for j in range(inner // LANES):
        lo, hi = j * LANES, (j + 1) * LANES
        h = j * per
        x_conv, x_shift = conv(lo, hi)
        x_sig = jax.nn.sigmoid(x_conv)
        xs = x_conv * x_sig
        step = widen(sp.dt, h, lane, width)
        xdt = xs * step
        xdt_low = xdt.astype(BF16)
        grad = dy[0, :, lo:hi]
        grad_low = grad.astype(BF16)
        core = y[0, :, lo:hi] - dsk[:, lo:hi] * xs
        late = d_state[:, lo:hi]
        late_low = late.astype(BF16)
        early = st[0, 0, :, lo:hi]
        tail = widen(sp.tail, h, lane, width)
        lead = widen(sp.lead, h, lane, width)
        u = None
        for i in range(per):
            fade = sp.fade(h + i)
            here = (lane >= i * width) & (lane < (i + 1) * width)
            own = jnp.where(here, grad, 0.0).astype(BF16)
            d_scores = d_scores + mm(own, xdt_low, NT) * fade
            part = mm((fade * scores).astype(BF16), grad_low, TN)
            u = part if u is None else jnp.where(lane >= i * width, part, u)
        from_end = tail * mm(write, late_low)
        u = u + from_end
        weighted = (lead * grad).astype(BF16)
        d_read = d_read + mm(weighted, early.astype(BF16), NT)
        d_write = d_write + mm((xdt * tail).astype(BF16), late_low, NT)
        end_lead = widen(sp.lead[q - 1 : q], h, lane, width)
        d_state[:, lo:hi] = end_lead * late + mm(read_t, weighted)
        head_of = (
            lax.broadcasted_iota(jnp.int32, (LANES, LANES), 0) // width + h
            == lax.broadcasted_iota(jnp.int32, (LANES, LANES), 1)
        ).astype(F32)
        d_cum = d_cum + mm(grad * core - xdt * u, head_of, precision=PRECISE)
        d_step = d_step + mm(xs * u, head_of, precision=PRECISE)
        end_row = end_lead * jnp.sum(late * early, axis=0, keepdims=True) + jnp.sum(
            xdt * from_end, axis=0, keepdims=True
        )
        d_end = d_end + mm(jnp.broadcast_to(end_row, (8, LANES)), head_of, precision=PRECISE)
        acc[taps + 1 : taps + 2, lo:hi] += jnp.sum(grad * xs, axis=0, keepdims=True)
        unconv(lo, hi, step * u + dsk[:, lo:hi] * grad, x_conv, x_shift, x_sig)
    d_low = d_scores.astype(BF16)
    d_read = d_read + mm(d_low, write)
    d_write = d_write + mm(d_low, read, TN)
    unconv(inner, inner + n, d_write, w_conv, w_shift, w_sig)
    unconv(inner + n, inner + 2 * n, d_read, r_conv, r_shift, r_sig)
    d_decay = mm(sp.tri, d_cum, TN, precision=PRECISE) + d_end[0:1]
    acc_head[0:1] += jnp.sum(d_decay * sp.dt, axis=0, keepdims=True) * rate[...]
    d_dt = (d_step + d_decay * rate[...]) * jax.nn.sigmoid(sp.dt_in)
    acc_head[1:2] += jnp.sum(d_dt, axis=0, keepdims=True)
    ddt_out[0] = d_dt.astype(BF16)


def whole(shape):
    return pl.BlockSpec(shape, lambda *_: (0,) * len(shape))


def params():
    return pltpu.CompilerParams(vmem_limit_bytes=48 << 20)


def scan_forward(offs, pos, pre, rim, dtr, cw, cb, dtb, rate, dsk, width, n):
    nb, length, chans = pre.shape
    inner = dsk.shape[1]
    q = min(CHUNK, length)
    chunks = length // q
    dims = (q, inner, width, n)

    def rows(size):
        return pl.BlockSpec((1, q, size), lambda b, c, *_: (b, c, 0))

    return pl.pallas_call(
        functools.partial(scan_kernel, dims),
        grid_spec=pltpu.PrefetchScalarGridSpec(
            num_scalar_prefetch=2,
            grid=(nb, chunks),
            in_specs=[
                rows(chans),
                pl.BlockSpec((1, 8, chans), lambda b, c, *_: (b, 0, 0)),
                rows(LANES),
                whole(cw.shape),
                whole(cb.shape),
                whole(dtb.shape),
                whole(rate.shape),
                whole(dsk.shape),
            ],
            out_specs=[
                rows(inner),
                rows(n),
                rows(LANES),
                pl.BlockSpec((1, 1, n, inner), lambda b, c, *_: (b, c, 0, 0)),
                pl.BlockSpec((1, 1, 8, LANES), lambda b, c, *_: (b, c, 0, 0)),
                pl.BlockSpec((1, n, inner), lambda b, c, *_: (b, 0, 0)),
            ],
            scratch_shapes=[
                pltpu.VMEM((8, chans), F32),
                pltpu.VMEM((n, inner), F32),
                pltpu.VMEM((1, LANES), F32),
            ],
        ),
        out_shape=[
            jax.ShapeDtypeStruct((nb, length, inner), F32),
            jax.ShapeDtypeStruct((nb, length, n), BF16),
            jax.ShapeDtypeStruct((nb, length, LANES), F32),
            jax.ShapeDtypeStruct((nb, chunks, n, inner), F32),
            jax.ShapeDtypeStruct((nb, chunks, 8, LANES), F32),
            jax.ShapeDtypeStruct((nb, n, inner), F32),
        ],
        compiler_params=params(),
        name="scan_forward",
    )(offs, pos, pre, rim, dtr, cw, cb, dtb, rate, dsk)


def gate_forward(y_in, rd, lead, lead0, st, s_in, z, gain, width):
    nb, length, inner = y_in.shape
    chunks, n = st.shape[1], st.shape[2]
    q = length // chunks
    dims = (q, inner, width, n)

    def rows(size):
        return pl.BlockSpec((1, q, size), lambda b, c: (b, c, 0))

    def per_chunk(r, size):
        return pl.BlockSpec((1, 1, r, size), lambda b, c: (b, c, 0, 0))

    return pl.pallas_call(
        functools.partial(gate_kernel, dims),
        grid=(nb, chunks),
        in_specs=[
            rows(inner),
            rows(n),
            rows(LANES),
            per_chunk(8, LANES),
            per_chunk(n, inner),
            pl.BlockSpec((1, n, inner), lambda b, c: (b, 0, 0)),
            rows(inner),
            whole(gain.shape),
        ],
        out_specs=[rows(inner), rows(inner), rows(LANES), per_chunk(n, inner)],
        out_shape=[
            jax.ShapeDtypeStruct((nb, length, inner), F32),
            jax.ShapeDtypeStruct((nb, length, inner), BF16),
            jax.ShapeDtypeStruct((nb, length, LANES), F32),
            jax.ShapeDtypeStruct(st.shape, F32),
        ],
        compiler_params=params(),
        name="gate_forward",
    )(y_in, rd, lead, lead0, st, s_in, z, gain)


def gate_backward(dyn, y, z, stat, gain, rd, lead, width, count):
    nb, length, inner = y.shape
    n = rd.shape[2]
    q = min(CHUNK, length)
    chunks = length // q
    dims = (q, inner, width, n)

    def rows(size):
        return pl.BlockSpec((1, q, size), lambda b, c: (b, c, 0))

    return pl.pallas_call(
        functools.partial(ungate_kernel, dims, count),
        grid=(nb, chunks),
        in_specs=[
            rows(inner),
            rows(inner),
            rows(inner),
            rows(LANES),
            whole(gain.shape),
            rows(n),
            rows(LANES),
        ],
        out_specs=[
            rows(inner),
            rows(inner),
            rows(inner),
            whole((8, inner)),
            pl.BlockSpec((1, n, inner), lambda b, c: (b, 0, 0)),
        ],
        out_shape=[
            jax.ShapeDtypeStruct((nb, length, inner), F32),
            jax.ShapeDtypeStruct((nb, length, inner), BF16),
            jax.ShapeDtypeStruct((nb, length, inner), BF16),
            jax.ShapeDtypeStruct((8, inner), F32),
            jax.ShapeDtypeStruct((nb, n, inner), F32),
        ],
        compiler_params=params(),
        name="gate_backward",
    )(dyn, y, z, stat, gain, rd, lead)


def scan_backward(offs, pos, pre, rim, dtr, y, dy, st, d_in, cw, cb, dtb, rate, dsk, width):
    nb, length, chans = pre.shape
    inner = dsk.shape[1]
    chunks, n = st.shape[1], st.shape[2]
    q = length // chunks
    dims = (q, inner, width, n)
    per = q // 16

    def rows(size):
        return pl.BlockSpec((1, q, size), lambda b, c, *_: (b, chunks - 1 - c, 0))

    def per_seq(r, size):
        return pl.BlockSpec((1, r, size), lambda b, c, *_: (b, 0, 0))

    return pl.pallas_call(
        functools.partial(back_kernel, dims),
        grid_spec=pltpu.PrefetchScalarGridSpec(
            num_scalar_prefetch=2,
            grid=(nb, chunks),
            in_specs=[
                rows(chans),
                pl.BlockSpec(
                    (1, 16, chans), lambda b, c, *_: (b, jnp.maximum((chunks - 1 - c) * per - 1, 0), 0)
                ),
                per_seq(8, chans),
                rows(LANES),
                rows(inner),
                rows(inner),
                pl.BlockSpec((1, 1, n, inner), lambda b, c, *_: (b, chunks - 1 - c, 0, 0)),
                per_seq(n, inner),
                whole(cw.shape),
                whole(cb.shape),
                whole(dtb.shape),
                whole(rate.shape),
                whole(dsk.shape),
            ],
            out_specs=[
                rows(chans),
                rows(LANES),
                per_seq(8, chans),
                per_seq(8, chans),
                whole((8, chans)),
                whole((8, LANES)),
            ],
            scratch_shapes=[pltpu.VMEM((n, inner), F32), pltpu.VMEM((8, chans), F32)],
        ),
        out_shape=[
            jax.ShapeDtypeStruct((nb, length, chans), BF16),
            jax.ShapeDtypeStruct((nb, length, LANES), BF16),
            jax.ShapeDtypeStruct((nb, 8, chans), F32),
            jax.ShapeDtypeStruct((nb, 8, chans), F32),
            jax.ShapeDtypeStruct((8, chans), F32),
            jax.ShapeDtypeStruct((8, LANES), F32),
        ],
        compiler_params=params(),
        name="scan_backward",
    )(offs, pos, pre, pre, rim, dtr, y, dy, st, d_in, cw, cb, dtb, rate, dsk)


def shift(arr, axis, by):
    peers = lax.axis_size(axis)
    pairs = [(i, i + by) for i in range(peers) if 0 <= i + by < peers]
    return lax.ppermute(arr, axis, pairs)


def heads_row(vec, width=LANES):
    return jnp.pad(vec[None], ((0, 0), (0, width - vec.shape[0])))


def on_device(
    x_in,
    cotangent,
    offsets,
    in_gain,
    w_z,
    w_x,
    w_dt,
    w_bc,
    conv_w,
    conv_b,
    dt_bias,
    a_log,
    d_skip,
    norm_gain,
    w_out,
):
    batches, seq_count, length, width_dev = x_in.shape
    nb = batches * seq_count
    tokens = nb * length
    tp_rank = lax.axis_index("tp")
    ctx_rank = lax.axis_index("ctx")
    peers = lax.axis_size("ctx")
    inner = w_z.shape[1]
    heads = w_dt.shape[1]
    width = inner // heads
    model = in_gain.shape[0]
    inner_all = norm_gain.shape[0]
    pair = conv_w.shape[1] - inner_all
    n = pair // 2
    taps = conv_w.shape[0]

    def mine(arr, size, axis):
        return lax.dynamic_slice_in_dim(arr, tp_rank * size, size, axis)

    cw = jnp.concatenate([mine(conv_w, inner, 1), conv_w[:, inner_all:]], axis=1)
    cb = jnp.concatenate([mine(conv_b, inner, 0), conv_b[inner_all:]])[None]
    gain = mine(norm_gain, inner, 0)[None]
    gain_in = mine(in_gain, width_dev, 0)
    dtb = heads_row(mine(dt_bias, heads, 0))
    rate = heads_row(-jnp.exp(mine(a_log, heads, 0)))
    dsk = jnp.repeat(mine(d_skip, heads, 0), width)[None]
    pos = (ctx_rank * length).astype(jnp.int32)[None]
    offs = offsets.reshape(nb, offsets.shape[-1])

    x_own = x_in.reshape(tokens, width_dev)
    cot_own = cotangent.reshape(tokens, width_dev)
    x_all = lax.all_gather(x_own, "tp", axis=1, tiled=True)
    small = jnp.concatenate([w_bc, w_dt], axis=1)
    small = lax.all_gather(small, "fsdp", axis=0, tiled=True)
    wdt = jnp.pad(small[:, pair // lax.axis_size("tp") :], ((0, 0), (0, LANES - heads)))
    wbc = lax.all_gather(small[:, : pair // lax.axis_size("tp")], "tp", axis=1, tiled=True)
    wx = lax.all_gather(w_x, "fsdp", axis=0, tiled=True)
    wz = lax.all_gather(w_z, "fsdp", axis=0, tiled=True)
    wo = lax.all_gather(w_out, "fsdp", axis=1, tiled=True)
    cot_all = lax.all_gather(cot_own, "tp", axis=1, tiled=True)
    wxbc = jnp.concatenate([wx, wbc], axis=1)

    resid = x_all.astype(F32)
    r1 = lax.rsqrt(jnp.mean(resid * resid, axis=1, keepdims=True) + EPSILON)
    xn = (resid * r1 * in_gain).astype(BF16)
    pre = mm(xn, wxbc).astype(BF16).reshape(nb, length, inner + pair)
    dtr = mm(xn, wdt).reshape(nb, length, LANES)
    z = mm(xn, wz).reshape(nb, length, inner)
    rim = shift(pre[:, length - 8 :], "ctx", 1).astype(F32)
    y, rd, lead, st, lead0, fin = scan_forward(
        offs, pos, pre, rim, dtr, cw, cb, dtb, rate, dsk, width, n
    )
    lend = jnp.repeat(lead[:, length - 1, :heads], width, axis=-1)[:, None]

    def chained(start, by):
        came = jnp.zeros_like(start)
        for k in range(peers - 1):
            sent = start if k == 0 else start + lend * came
            came = shift(sent.astype(BF16), "ctx", by).astype(F32)
        return came

    s_in = chained(fin, 1)
    y, ygg, sq, st = gate_forward(y, rd, lead, lead0, st, s_in, z, gain, width)
    part = mm(ygg.reshape(tokens, inner), wo).astype(BF16)
    share = lax.psum_scatter(part, "tp", scatter_dimension=1, tiled=True)
    dyn = mm(cot_all, wo, NT).reshape(nb, length, inner)
    dot = jnp.sum(dyn * gain * y * jax.nn.silu(z), axis=2)
    stat = jnp.stack([sq[..., 0], dot])
    stat = jnp.sum(lax.all_gather(stat, "tp"), axis=0)
    r2 = lax.rsqrt(stat[0] / inner_all + EPSILON)
    out = x_own.astype(F32) + r2.reshape(tokens, 1) * share.astype(F32)
    stat = jnp.pad(jnp.stack([r2, stat[1]], axis=-1), ((0, 0), (0, 0), (0, LANES - 2)))
    dy, dz, yn, g_gain, g_state = gate_backward(dyn, y, z, stat, gain, rd, lead, width, inner_all)
    dz = dz.reshape(tokens, inner)
    yn = yn.reshape(tokens, inner)
    d_in = chained(g_state, -1)
    rows = ("ctx", "fsdp")

    def scattered(grad):
        return lax.psum_scatter(grad.astype(BF16), rows, scatter_dimension=0, tiled=True)

    g_out = scattered(mm(cot_all, yn, TN)).astype(F32).T
    g_z = scattered(mm(xn, dz, TN)).astype(F32)
    dcat, ddt, edge, rim_grad, acc, acc_head = scan_backward(
        offs, pos, pre, rim, dtr, y, dy, st, d_in, cw, cb, dtb, rate, dsk, width
    )
    edge = (edge + shift(rim_grad, "ctx", -1)).astype(BF16)
    dcat = lax.dynamic_update_slice(dcat, edge, (0, length - 8, 0)).reshape(tokens, inner + pair)
    ddt = ddt.reshape(tokens, LANES)
    dxn = mm(dz, wz, NT) + mm(dcat, wxbc, NT) + mm(ddt, wdt, NT)
    dxn = lax.psum_scatter(dxn.astype(BF16), "tp", scatter_dimension=1, tiled=True).astype(F32)
    g_xbc = scattered(jnp.concatenate([mm(xn, dcat, TN), mm(xn, ddt, TN)[:, :heads]], axis=1))
    g_x = g_xbc[:, :inner].astype(F32)
    g_dt = g_xbc[:, inner + pair :].astype(F32)
    g_bc = lax.psum_scatter(
        g_xbc[:, inner : inner + pair].astype(F32), "tp", scatter_dimension=1, tiled=True
    )
    h_own = x_own.astype(F32)
    scaled = dxn * gain_in
    in_dot = jnp.sum(lax.all_gather(jnp.sum(scaled * h_own, axis=1), "tp"), axis=0)[:, None]
    g_in = jnp.sum(dxn * h_own * r1, axis=0)
    d_x = cot_own.astype(F32) + r1 * scaled - h_own * r1**3 * in_dot / model
    pieces = [
        g_in,
        acc[:taps, :inner].reshape(-1),
        acc[taps, :inner],
        g_gain[0],
        acc_head[1, :heads],
        acc_head[0, :heads],
        acc[taps + 1, :inner].reshape(heads, width).sum(axis=1),
        acc[:taps, inner:].reshape(-1),
        acc[taps, inner:],
    ]
    sizes = [p.shape[0] for p in pieces]
    packed = jnp.sum(lax.all_gather(jnp.concatenate(pieces), rows), axis=0)
    packed = lax.all_gather(packed, "tp")
    parts, start = [], 0
    for size in sizes:
        parts.append(packed[:, start : start + size])
        start += size
    tp = packed.shape[0]
    g_cw = jnp.concatenate(
        [
            parts[1].reshape(tp, taps, inner).transpose(1, 0, 2).reshape(taps, inner_all),
            jnp.sum(parts[7], axis=0).reshape(taps, pair),
        ],
        axis=1,
    )
    g_cb = jnp.concatenate([parts[2].reshape(-1), jnp.sum(parts[8], axis=0)])
    shape = (batches, seq_count, length, width_dev)
    return (
        out.reshape(shape),
        d_x.reshape(shape),
        parts[0].reshape(-1),
        g_z,
        g_x,
        g_dt,
        g_bc,
        g_cw,
        g_cb,
        parts[4].reshape(-1),
        parts[5].reshape(-1),
        parts[6].reshape(-1),
        parts[3].reshape(-1),
        g_out,
    )


def solution(mesh):
    stream = P(None, "fsdp", "ctx", "tp")
    weight = P("fsdp", "tp")
    grad = P(("ctx", "fsdp"), "tp")
    in_specs = (
        (stream, stream, P(None, "fsdp", None), P())
        + (weight,) * 4
        + (P(),) * 6
        + (P("tp", "fsdp"),)
    )
    out_specs = (
        (stream, stream, P()) + (grad,) * 4 + (P(),) * 6 + (P("tp", ("ctx", "fsdp")),)
    )
    return jax.shard_map(
        on_device, mesh=mesh, in_specs=in_specs, out_specs=out_specs, check_vma=False
    )
```

time: 1670 us -> 909 us (0.54)
  local copies, waits for them, and re-layouts: 303 us -> 18.8 us
  matrix products: 303 us -> 81.7 us
  waiting for transfers between devices: 782 us -> 615 us
  other arithmetic: 137 us -> 28.3 us
  Pallas kernels: 0 us -> 95 us
  blocking collectives: 97 us -> 34.3 us
    reduce_scatter x9 -> x6, waiting for transfers between devices: 510 us -> 271 us  [the longest x3 153 us: scattered(): lax.psum_scatter(grad.astype(BF16), rows, scatter_dimension=0, tiled=True)]
    dot_general x92 -> x12, matrix products: 303 us -> 81.7 us  [mm(): lax.dot_general(a, b, (dims, ((), ())), precision=precision, preferred_el...]
    psum x1 -> x0, waiting for transfers between devices: 119 us -> none  [on_device(): lax.psum((small_sums[0], small_sums[1], small_sums[2], small_sums[3], sma...]
    dynamic_update_slice x32 -> x0, local copies, waits for them, and re-layouts: 101 us -> none  [the longest x24 99.8 us: local_scan(): lax.scan(jax.checkpoint(stretch_step), start_state, (blocked(values), blo...]
    pallas_call x0 -> x4, Pallas kernels: none -> 95 us  [the longest x1 54.5 us: scan_backward(): pl.pallas_call(functools.partial(back_kernel, dims), grid_spec=pltpu.Pref...]
    all_gather x12 -> x6, waiting for transfers between devices: 149 us -> 243 us  [the longest x1 79.6 us: on_device(): x_all = lax.all_gather(x_own, 'tp', axis=1, tiled=True)]
    unnamed x26 -> x16, waiting for transfers between devices: 3.31 us -> 89 us
    psum x4 -> x0, blocking collectives: 75.7 us -> none  [the longest x1 43.6 us: on_device(): lax.psum((small_sums[0], small_sums[1], small_sums[2], small_sums[3], sma...]
  transfers between devices with their start and end apart: 28 -> 18, of which waited for: 16 -> 15; matrix products, arithmetic and copies ran while one was open for 28% -> 12% of each run, Pallas kernels for 0% -> 2%
where the time goes in v1:
time: 909 us; the launch traced here: 900 us
  waiting for transfers between devices  615 us (68%)
  Pallas kernels  95 us (10%)
  matrix products  81.7 us (9%)
  blocking collectives  34.3 us (4%)
  other arithmetic  28.3 us (3%)
  local copies, waits for them, and re-layouts  18.8 us (2%)
  between operations  16.4 us (2%)
  starting transfers between devices  11 us (1%)
    reduce_scatter x3, waiting for transfers between devices, scattered(): lax.psum_scatter(grad.astype(BF16), rows, scatter_dimension=0, tiled=True)  153 us
    unnamed x16, waiting for transfers between devices  89 us
    dot_general x12, matrix products, mm(): lax.dot_general(a, b, (dims, ((), ())), precision=precision, preferred_el...  81.7 us
    all_gather x1, waiting for transfers between devices, on_device(): x_all = lax.all_gather(x_own, 'tp', axis=1, tiled=True)  79.6 us
    reduce_scatter x1, waiting for transfers between devices, on_device(): share = lax.psum_scatter(part, 'tp', scatter_dimension=1, tiled=True)  59.4 us
    pallas_call x1, Pallas kernels, scan_backward(): pl.pallas_call(functools.partial(back_kernel, dims), grid_spec=pltpu.Pref...  54.5 us
    all_gather x1, waiting for transfers between devices, on_device(): cot_all = lax.all_gather(cot_own, 'tp', axis=1, tiled=True)  49.4 us
    reduce_scatter x1, waiting for transfers between devices, on_device(): lax.psum_scatter(dxn.astype(BF16), 'tp', scatter_dimension=1, tiled=True)  42.3 us
  transfers between devices with their start and end apart: 18, of which 15 were waited for; matrix products, arithmetic and copies ran while one was open for 12% of the time, Pallas kernels for 2%

profile of v1, /device:TPU:0, one launch (start us, length us, event | category | flops | bytes accessed | tf_op | source)
XLA Modules:
  0.0 900.5 jit_solution(17261915752596390653)
XLA Ops:
  8.2 7.6 all_gather.47
  21.0 24.7 %all-gather.15.cloned.1.call-done = bf16[2048,256]{0,1:T(8,128)(2,1)} async-done(((bf16[2048,64]{0,1:T(8,128)(2,1)}), bf16[2048,256]{0,1:T(8,128)(2,1)}) %all-gather.15.cloned.1.call-update) | async-done | bytes 1048592 | tf_op jit(solution)/shard_map/all_gather | solution.py:582
  45.7 2.3 copy.56
  47.9 79.6 %all-gather.11.cloned.1.call-done = bf16[1024,2048]{1,0:T(8,128)(2,1)} async-done(((bf16[1024,512]{1,0:T(8,128)(2,1)}), bf16[1024,2048]{1,0:T(8,128)(2,1)}) %all-gather.11.cloned.1.call-update) | async-done | bytes 4194320 | tf_op jit(solution)/shard_map/all_gather | solution.py:578
  127.5 3.1 fusion
  130.6 31.5 %all-gather.13.cloned.1.call-done = bf16[2048,1024]{1,0:T(8,128)(2,1)} async-done(((bf16[512,1024]{1,0:T(8,128)(2,1)}), bf16[2048,1024]{1,0:T(8,128)(2,1)}) %all-gather.13.cloned.1.call-update) | async-done | bytes 4194320 | tf_op jit(solution)/shard_map/all_gather | solution.py:583
  162.2 9.2 %convolution_convert_fusion.1 = bf16[1024,1280]{1,0:T(8,128)(2,1)S(1)} fusion(bf16[2048,256]{1,0:T(8,128)(2,1)} %copy.56, bf16[2048,1024]{1,0:T(8,128)(2,1)} %all-gather.13.cloned.1.call-done, bf16[1024,2048]{1,0:T(8,128)(2,1)} %all-gather.11.cloned.1.call-done, f32[2048]{0:T(1024)S(1)} %copy-done.25, f32[1024]{0:T(1024)S(1)} %get-tuple-element.144), kind=kOutput, calls=%fused_computation.11 | convolution fusion | flops 5388894208 | bytes 12070912 | tf_op jit(solution)/shard_map/dot_general | solution.py:20
  171.4 3.4 collective-permute-start
  174.8 23.3 %all-gather.17.cloned.1.call-done = bf16[2048,1024]{1,0:T(8,128)(2,1)} async-done(((bf16[512,1024]{1,0:T(8,128)(2,1)}), bf16[2048,1024]{1,0:T(8,128)(2,1)}) %all-gather.17.cloned.1.call-update) | async-done | bytes 4194320 | tf_op jit(solution)/shard_map/all_gather | solution.py:584
  198.1 10.2 %fusion.28 = f32[1024,1024]{1,0:T(8,128)} fusion(bf16[2048,1024]{1,0:T(8,128)(2,1)} %all-gather.17.cloned.1.call-done, bf16[1024,2048]{1,0:T(8,128)(2,1)} %all-gather.11.cloned.1.call-done, f32[2048]{0:T(1024)S(1)} %copy-done.25, f32[1024]{0:T(1024)S(1)} %get-tuple-element.144), kind=kOutput, calls=%fused_computation.76 | convolution fusion | flops 4303355904 | bytes 12595200 | tf_op jit(solution)/shard_map/dot_general | solution.py:20
  208.3 1.3 fusion.13
  209.7 16.7 %scan_forward.1 = (f32[2,512,1024]{2,1,0:T(8,128)}, bf16[2,512,128]{2,1,0:T(8,128)(2,1)S(1)}, f32[2,512,128]{2,1,0:T(8,128)S(1)}, f32[2,4,128,1024]{3,2,1,0:T(8,...) custom-call(s32[2,4]{1,0:T(2,128)S(1)} %bitcast.102, s32[1]{0:T(128)} %bitcast.2.pos, ...), custom_call_target="tpu_custom_call" | custom-call | tf_op jit(solution)/shard_map/scan_forward/pallas_call | solution.py:342
  227.1 3.9 collective-permute-start.1
  230.9 49.4 %all-gather.19.cloned.1.call-done = bf16[1024,2048]{1,0:T(8,128)(2,1)} async-done(((bf16[1024,512]{1,0:T(8,128)(2,1)}), bf16[1024,2048]{1,0:T(8,128)(2,1)}) %all-gather.19.cloned.1.call-update) | async-done | bytes 4194320 | tf_op jit(solution)/shard_map/all_gather | solution.py:586
  280.3 34.5 %all-gather.21.cloned.1.call-done = bf16[1024,2048]{1,0:T(8,128)(2,1)} async-done(((bf16[1024,512]{1,0:T(8,128)(2,1)}), bf16[1024,2048]{1,0:T(8,128)(2,1)}) %all-gather.21.cloned.1.call-update) | async-done | bytes 4194320 | tf_op jit(solution)/shard_map/all_gather | solution.py:585
  314.8 7.6 fusion.33
  322.5 13.1 %gate_forward.1 = (f32[2,512,1024]{2,1,0:T(8,128)}, bf16[2,512,1024]{2,1,0:T(8,128)(2,1)S(1)}, f32[2,512,128]{2,1,0:T(8,128)S(1)}, f32[2,4,128,1024]{3,2,1,0:T(8,128)}) custom-call(f32[2,512,1024]{2,1,0:T(8,128)} %get-tuple-element.35.y_in, bf16[2,512,128]{2,1,0:T(8,128)(2,1)S(1)} %get-tuple-element.36.rd, f32[2,512,128]{2,1,0:T(8,128)S(1)} %get-tuple-element.37.lead, ...), custom_call_target="tpu_custom_call" | custom-call | tf_op jit(solution)/shard_map/gate_forward/pallas_call | solution.py:396
  335.8 4.0 multiply_reduce_fusion
  339.9 13.2 %all-gather = f32[8,2,512]{2,1,0:T(2,128)S(1)} all-gather(f32[2,2,512]{2,1,0:T(2,128)S(1)} %pad_maximum_fusion.9), channel_id=2, replica_groups=mesh['ctx'=2,'tp'=4,'fsdp'=4] {'tp'}, dimensions={0}, use_global_device_ids=true | all-gather | bytes 40960 | tf_op jit(solution)/shard_map/all_gather | solution.py:615
  353.8 10.8 %gate_backward.1 = (f32[2,512,1024]{2,1,0:T(8,128)}, bf16[2,512,1024]{2,1,0:T(8,128)(2,1)S(1)}, bf16[2,512,1024]{2,1,0:T(8,128)(2,1)}, f32[8,1024]{1,0:T(8,128)S(1)}, f32[2,128,1024]{2,1,0:T(8,128)S(1)}) custom-call(f32[2,512,1024]{2,1,0:T(8,128)} %bitcast.113, f32[2,512,1024]{2,1,0:T(8,128)} %get-tuple-element.42.y, f32[2,512,1024]{2,1,0:T(8,128)} %bitcast.110, ...), custom_call_target="tpu_custom_call" | custom-call | tf_op jit(solution)/shard_map/gate_backward/pallas_call | solution.py:431
  365.9 11.8 %collective-permute-done.2 = bf16[2,128,1024]{2,1,0:T(8,128)(2,1)S(1)} collective-permute-done((bf16[2,128,1024]{2,1,0:T(8,128)(2,1)S(1)}, bf16[2,128,1024]{2,1,0:T(8,128)(2,1)S(1)}, u32[]{:S(2)}, u32[]{:S(2)}) %collective-permute-start.2) | collective-permute-done | bytes 524320 | tf_op jit(solution)/shard_map/ppermute | solution.py:524
  377.8 54.5 %scan_backward.1 = (bf16[2,512,1280]{2,1,0:T(8,128)(2,1)S(1)}, bf16[2,512,128]{2,1,0:T(8,128)(2,1)S(1)}, f32[2,8,1280]{2,1,0:T(8,128)S(1)}, f32[2,8,1280]{2,1,0:...) custom-call(s32[2,4]{1,0:T(2,128)S(1)} %bitcast.103, s32[1]{0:T(128)} %bitcast.2.pos, ...), custom_call_target="tpu_custom_call" | custom-call | tf_op jit(solution)/shard_map/scan_backward/pallas_call | solution.py:476
  432.3 1.5 collective-permute-start.3
  433.8 6.5 fusion.34
  440.4 5.6 fusion.3
  446.0 3.3 add_convert_fusion
  450.0 9.8 %convolution_convert_fusion.2 = bf16[2048,1024]{1,0:T(8,128)(2,1)} fusion(bf16[1024,1024]{1,0:T(8,128)(2,1)} %bitcast.108, bf16[1024,2048]{1,0:T(8,128)(2,1)} %all-gather.11.cloned.1.call-done, f32[2048]{0:T(1024)S(1)} %copy-done.26, f32[1024]{0:T(1024)S(1)} %get-tuple-element.144), kind=kOutput, calls=%fused_computation.12 | convolution fusion | flops 4305453056 | bytes 10498048 | tf_op jit(solution)/shard_map/dot_general | solution.py:20
  460.0 9.4 %convert_bitcast_fusion = bf16[2048,1024]{0,1:T(8,128)(2,1)} fusion(bf16[1024,1024]{1,0:T(8,128)(2,1)} %bitcast.132, bf16[1024,2048]{1,0:T(8,128)(2,1)} %all-gather.19.cloned.1.call-done), kind=kOutput, calls=%fused_computation.9 | convolution fusion | flops 4297064448 | bytes 10485760 | tf_op jit(solution)/shard_map/dot_general | solution.py:20
  469.6 3.8 fusion.24
  473.3 6.7 convolution_convert_fusion
  480.0 2.9 pad_maximum_fusion
  485.1 42.3 %reduce-scatter.9.cloned.1.call-done = bf16[1024,512]{1,0:T(8,128)(2,1)} async-done(((bf16[1024,2048]{1,0:T(8,128)(2,1)}), bf16[1024,512]{1,0:T(8,128)(2,1)}) %reduce-scatter.9.cloned.1.call-update) | async-done | bytes 1048592 | tf_op jit(solution)/shard_map/reduce_scatter | solution.py:637
  527.4 2.2 fusion.11
  531.3 8.3 convolution_convert_fusion.3
  541.5 41.5 %reduce-scatter.11.cloned.1.call-done = bf16[256,1024]{1,0:T(8,128)(2,1)} async-done(((bf16[2048,1024]{1,0:T(8,128)(2,1)}), bf16[256,1024]{1,0:T(8,128)(2,1)}) %reduce-scatter.11.cloned.1.call-update) | async-done | bytes 524304 | tf_op jit(solution)/shard_map/reduce_scatter | solution.py:626
  583.0 2.1 convert_element_type.92
  585.1 52.6 %reduce-scatter.17.cloned.1.call-done = bf16[256,1024]{0,1:T(8,128)(2,1)} async-done(((bf16[2048,1024]{0,1:T(8,128)(2,1)}), bf16[256,1024]{0,1:T(8,128)(2,1)}) %reduce-scatter.17.cloned.1.call-update) | async-done | bytes 524304 | tf_op jit(solution)/shard_map/reduce_scatter | solution.py:626
  637.7 2.1 convert_bitcast_fusion.1
  639.8 59.0 %reduce-scatter.13.cloned.1.call-done = bf16[256,1296]{0,1:T(8,128)(2,1)} async-done(((bf16[2048,1296]{0,1:T(8,128)(2,1)}), bf16[256,1296]{0,1:T(8,128)(2,1)}) %reduce-scatter.13.cloned.1.call-update) | async-done | bytes 663568 | tf_op jit(solution)/shard_map/reduce_scatter | solution.py:626
  698.8 2.1 slice_convert_fusion
  700.9 2.5 copy.62
  703.4 52.3 %all-reduce.9.cloned.1.call-done = f32[63872]{0:T(1024)} async-done(((f32[63872]{0:T(1024)}), f32[63872]{0:T(1024)}) %all-reduce.9.cloned.1.call-update) | async-done | bytes 255504
  758.2 1.6 slice_convert_fusion.1
  761.2 13.6 %all-gather.1 = f32[4096]{0:T(1024)S(1)} all-gather(f32[1024]{0:T(1024)S(1)} %get-tuple-element.127), channel_id=3, replica_groups=mesh['ctx'=2,'tp'=4,'fsdp'=4] {'tp'}, dimensions={0}, use_global_device_ids=true | all-gather | bytes 20480 | tf_op jit(solution)/shard_map/all_gather | solution.py:646
  774.8 59.4 %reduce-scatter.7.cloned.1.call-done = bf16[1024,512]{1,0:T(8,128)(2,1)} async-done(((bf16[1024,2048]{1,0:T(8,128)(2,1)}), bf16[1024,512]{1,0:T(8,128)(2,1)}) %reduce-scatter.7.cloned.1.call-update) | async-done | bytes 1048592 | tf_op jit(solution)/shard_map/reduce_scatter | solution.py:611
  834.2 3.7 fusion.6
  837.9 33.6 %all-reduce.11.cloned.1.call-done = f32[31936]{0:T(1024)} async-done(((f32[31936]{0:T(1024)}), f32[31936]{0:T(1024)}) %all-reduce.11.cloned.1.call-update) | async-done | bytes 127760
  877.1 16.4 %reduce-scatter.15.cloned.1.call-done = f32[256,64]{0,1:T(8,128)} async-done(((f32[256,256]{0,1:T(8,128)}), f32[256,64]{0,1:T(8,128)}) %reduce-scatter.15.cloned.1.call-update) | async-done | bytes 65552 | tf_op jit(solution)/shard_map/reduce_scatter | solution.py:641
  (169 shorter events, 24.0 us)
Async XLA Ops:
  7.2 13.8 %copy-start.21 = (f32[4,4352]{1,0:T(4,128)S(1)}, f32[4,4352]{1,0:T(4,128)}, u32[]{:S(2)}) copy-start(f32[4,4352]{1,0:T(4,128)} %param.23) | copy-start | bytes 208900
  7.2 13.8 %slice-start = ((f32[4,4352]{1,0:T(4,128)}), f32[4,256]{1,0:T(4,128)S(1)}, s32[]{:S(2)}) async-start(f32[4,4352]{1,0:T(4,128)} %param.23), calls=%async_computation.20 | async-start | bytes 8192 | tf_op jit(solution)/shard_map/slice | solution.py:566
  7.2 12.6 %copy-start.22 = (f32[4352]{0:T(1024)S(1)}, f32[4352]{0:T(1024)}, u32[]{:S(2)}) copy-start(f32[4352]{0:T(1024)} %param.24) | copy-start | bytes 52228
  7.2 12.7 %slice-start.1 = ((f32[4352]{0:T(1024)}), f32[256]{0:T(256)S(1)}, s32[]{:S(2)}) async-start(f32[4352]{0:T(1024)} %param.24), calls=%async_computation.21 | async-start | bytes 2048 | tf_op jit(solution)/shard_map/slice | solution.py:567
  7.2 12.7 %copy-start.24 = (f32[64]{0:T(128)S(1)}, f32[64]{0:T(128)}, u32[]{:S(2)}) copy-start(f32[64]{0:T(128)} %param.25) | copy-start | bytes 772
  7.2 12.7 %copy-start.23 = (f32[64]{0:T(128)S(1)}, f32[64]{0:T(128)}, u32[]{:S(2)}) copy-start(f32[64]{0:T(128)} %param.26) | copy-start | bytes 772
  7.2 12.8 %copy-start.28 = (f32[64]{0:T(128)S(1)}, f32[64]{0:T(128)}, u32[]{:S(2)}) copy-start(f32[64]{0:T(128)} %param.27) | copy-start | bytes 772
  7.3 38.4 %all-gather.15.cloned.1.call-start = ((), (), s32[]{:S(2)}) async-start(), calls=%async_computation.8 | async-start | bytes 1310720 | tf_op jit(solution)/shard_map/all_gather | solution.py:582
  16.5 111.1 %all-gather.11.cloned.1.call-start = ((), (), s32[]{:S(2)}) async-start(), calls=%async_computation.6 | async-start | bytes 5242880 | tf_op jit(solution)/shard_map/all_gather | solution.py:578
  17.2 144.9 %all-gather.13.cloned.1.call-start = ((), (), s32[]{:S(2)}) async-start(), calls=%async_computation.7 | async-start | bytes 5242880 | tf_op jit(solution)/shard_map/all_gather | solution.py:583
  18.0 180.1 %all-gather.17.cloned.1.call-start = ((), (), s32[]{:S(2)}) async-start(), calls=%async_computation.9 | async-start | bytes 5242880 | tf_op jit(solution)/shard_map/all_gather | solution.py:584
  18.5 261.8 %all-gather.19.cloned.1.call-start = ((), (), s32[]{:S(2)}) async-start(), calls=%async_computation.10 | async-start | bytes 5242880 | tf_op jit(solution)/shard_map/all_gather | solution.py:586
  18.6 143.6 %copy-start.25 = (f32[2048]{0:T(1024)S(1)}, f32[2048]{0:T(1024)}, u32[]{:S(2)}) copy-start(f32[2048]{0:T(1024)} %param.18) | copy-start | bytes 24580
  19.1 295.6 %all-gather.21.cloned.1.call-start = ((), (), s32[]{:S(2)}) async-start(), calls=%async_computation.11 | async-start | bytes 5242880 | tf_op jit(solution)/shard_map/all_gather | solution.py:585
  19.7 507.7 %reduce-scatter.9.cloned.1.call-start = ((), (), s32[]{:S(2)}) async-start(), calls=%async_computation.13 | async-start | bytes 5242880 | tf_op jit(solution)/shard_map/reduce_scatter | solution.py:637
  19.8 188.6 %copy-start.19 = (bf16[2048,16]{0,1:T(8,128)(2,1)}, bf16[2048,16]{0,1:T(8,128)(2,1)S(1)}, u32[]{:S(2)}) copy-start(bf16[2048,16]{0,1:T(8,128)(2,1)S(1)} %slice.119) | copy-start | bytes 196612
  171.4 38.3 %copy-start = (bf16[1024,1280]{1,0:T(8,128)(2,1)}, bf16[1024,1280]{1,0:T(8,128)(2,1)S(1)}, u32[]{:S(2)}) copy-start(bf16[1024,1280]{1,0:T(8,128)(2,1)S(1)} %convolution_convert_fusion.1) | copy-start | bytes 7864324
  171.4 38.3 %collective-permute-start = (bf16[2,8,1280]{2,1,0:T(8,128)(2,1)S(1)}, bf16[2,8,1280]{2,1,0:T(8,128)(2,1)S(1)}, u32[]{:S(2)}, u32[]{:S(2)}) collective-permute-start(bf16[2,8,1280]{2,1,0:T(8,128)(2,1)S(1)} %slice.118), channel_id=1, source_target_pairs={{0,16},{1,17},{2,18},{3,19},{4,20},{5,21},{6,22},{7,23},{8,24},{9,... | collective-permute-start | bytes 122888 | tf_op jit(solution)/shard_map/ppermute | solution.py:524
  198.1 10.2 %copy-start.14 = (bf16[1024,2048]{1,0:T(8,128)(2,1)S(1)}, bf16[1024,2048]{1,0:T(8,128)(2,1)}, u32[]{:S(2)}) copy-start(bf16[1024,2048]{1,0:T(8,128)(2,1)} %all-gather.11.cloned.1.call-done) | copy-start | bytes 12582916
  208.3 1.4 copy-start.5
  209.7 16.8 %copy-start.1 = (f32[1024,128]{1,0:T(8,128)}, f32[1024,128]{1,0:T(8,128)S(1)}, u32[]{:S(2)}) copy-start(f32[1024,128]{1,0:T(8,128)S(1)} %fusion.13) | copy-start | bytes 1572868
  227.1 95.3 %collective-permute-start.1 = (bf16[2,128,1024]{2,1,0:T(8,128)(2,1)S(1)}, bf16[2,128,1024]{2,1,0:T(8,128)(2,1)S(1)}, u32[]{:S(2)}, u32[]{:S(2)}) collective-permute-start(bf16[2,128,1024]{2,1,0:T(8,128)(2,1)S(1)} %convert_element_type.81), channel_id=1, source_target_pairs={{0,16},{1,17},{2,18},{3,19},{4,20},{5,21},{6,22},{7,23},{8,24},{9,... | collective-permute-start | bytes 1572872 | tf_op jit(solution)/shard_map/ppermute | solution.py:524
  230.9 91.6 %copy-start.4 = (f32[2,4,8,128]{3,2,1,0:T(8,128)S(1)}, f32[2,4,8,128]{3,2,1,0:T(8,128)}, u32[]{:S(2)}) copy-start(f32[2,4,8,128]{3,2,1,0:T(8,128)} %copy-done.3) | copy-start | bytes 98308
  322.4 13.4 %copy-start.10 = (f32[1024,1024]{1,0:T(8,128)}, f32[1024,1024]{1,0:T(8,128)S(1)}, u32[]{:S(2)}) copy-start(f32[1024,1024]{1,0:T(8,128)S(1)} %fusion.33) | copy-start | bytes 12582916
  322.5 13.3 %copy-start.9 = (f32[1024,1024]{1,0:T(8,128)S(1)}, f32[1024,1024]{1,0:T(8,128)}, u32[]{:S(2)}) copy-start(f32[1024,1024]{1,0:T(8,128)} %fusion.28) | copy-start | bytes 12582916
  335.6 4.3 copy-start.6
  353.7 24.1 %copy-start.2 = (f32[1024,128]{1,0:T(8,128)S(1)}, f32[1024,128]{1,0:T(8,128)}, u32[]{:S(2)}) copy-start(f32[1024,128]{1,0:T(8,128)} %copy-done.1) | copy-start | bytes 1572868
  364.6 75.8 %copy-start.8 = (bf16[2,512,1024]{2,1,0:T(8,128)(2,1)}, bf16[2,512,1024]{2,1,0:T(8,128)(2,1)S(1)}, u32[]{:S(2)}) copy-start(bf16[2,512,1024]{2,1,0:T(8,128)(2,1)S(1)} %get-tuple-element.44) | copy-start | bytes 6291460
  364.6 13.1 %collective-permute-start.2 = (bf16[2,128,1024]{2,1,0:T(8,128)(2,1)S(1)}, bf16[2,128,1024]{2,1,0:T(8,128)(2,1)S(1)}, u32[]{:S(2)}, u32[]{:S(2)}) collective-permute-start(bf16[2,128,1024]{2,1,0:T(8,128)(2,1)S(1)} %convert_element_type.86), channel_id=1, source_target_pairs={{16,0},{17,1},{18,2},{19,3},{20,4},{21,5},{22,6},{23,7},{24,8},{25... | collective-permute-start | bytes 1572872 | tf_op jit(solution)/shard_map/ppermute | solution.py:524
  432.3 8.0 collective-permute-start.3
  433.8 6.6 copy-start.16
  433.8 6.6 copy-start.27
  440.4 5.7 copy-start.20
  449.3 0.7 copy-start.26
  449.3 133.7 %reduce-scatter.11.cloned.1.call-start = ((), (), s32[]{:S(2)}) async-start(), calls=%async_computation.14 | async-start | bytes 4718592 | tf_op jit(solution)/shard_map/reduce_scatter | solution.py:626
  459.8 177.9 %reduce-scatter.17.cloned.1.call-start = ((), (), s32[]{:S(2)}) async-start(), calls=%async_computation.17 | async-start | bytes 4718592 | tf_op jit(solution)/shard_map/reduce_scatter | solution.py:626
  469.5 229.3 %reduce-scatter.13.cloned.1.call-start = ((), (), s32[]{:S(2)}) async-start(), calls=%async_computation.15 | async-start | bytes 5971968 | tf_op jit(solution)/shard_map/reduce_scatter | solution.py:626
  469.5 3.8 copy-start.15
  482.9 44.5 %copy-start.11 = (bf16[2,1,512,512]{3,2,1,0:T(8,128)(2,1)S(1)}, bf16[2,1,512,512]{3,2,1,0:T(8,128)(2,1)}, u32[]{:S(2)}) copy-start(bf16[2,1,512,512]{3,2,1,0:T(8,128)(2,1)} %param.15) | copy-start | bytes 3145732
  482.9 48.4 %copy-start.7 = (bf16[2,512,1024]{2,1,0:T(8,128)(2,1)S(1)}, bf16[2,512,1024]{2,1,0:T(8,128)(2,1)}, u32[]{:S(2)}) copy-start(bf16[2,512,1024]{2,1,0:T(8,128)(2,1)} %copy-done.6) | copy-start | bytes 6291460
  482.9 272.7 %all-reduce.9.cloned.1.call-start = ((), (), s32[]{:S(2)}) async-start(), calls=%async_computation.18 | async-start | bytes 516096
  530.2 0.7 copy-start.17
  531.0 303.3 %reduce-scatter.7.cloned.1.call-start = ((), (), s32[]{:S(2)}) async-start(), calls=%async_computation.12 | async-start | bytes 5242880 | tf_op jit(solution)/shard_map/reduce_scatter | solution.py:611
  539.6 331.9 %all-reduce.11.cloned.1.call-start = ((), (), s32[]{:S(2)}) async-start(), calls=%async_computation.19 | async-start | bytes 262144
  541.5 292.7 %copy-start.12 = (bf16[2,1,512,512]{3,2,1,0:T(8,128)(2,1)S(1)}, bf16[2,1,512,512]{3,2,1,0:T(8,128)(2,1)}, u32[]{:S(2)}) copy-start(bf16[2,1,512,512]{3,2,1,0:T(8,128)(2,1)} %param.16) | copy-start | bytes 3145732
  541.5 292.7 %copy-start.13 = (bf16[1024,512]{1,0:T(8,128)(2,1)S(1)}, bf16[1024,512]{1,0:T(8,128)(2,1)}, u32[]{:S(2)}) copy-start(bf16[1024,512]{1,0:T(8,128)(2,1)} %reduce-scatter.9.cloned.1.call-done) | copy-start | bytes 3145732
  757.4 0.7 copy-start.18
  758.1 135.4 %reduce-scatter.15.cloned.1.call-start = ((), (), s32[]{:S(2)}) async-start(), calls=%async_computation.16 | async-start | bytes 327680 | tf_op jit(solution)/shard_map/reduce_scatter | solution.py:641
  (3 other events, 1.9 us)
Sparse Core Ops, SparseCore 0:
  16.6 29.0 all-gather.14
  47.3 80.2 all-gather.10
  129.1 33.0 all-gather.12
  163.6 34.4 all-gather.16
  199.5 80.7 all-gather.18
  281.7 33.0 all-gather.20
  449.4 77.9 reduce-scatter.8
  531.1 51.8 reduce-scatter.10
  586.4 51.2 reduce-scatter.16
  641.5 57.2 reduce-scatter.12
  702.1 53.4 all-reduce.8
  757.8 76.3 reduce-scatter.6
  836.6 34.8 all-reduce.10
  874.2 19.2 reduce-scatter.14

commit v2 on v1

--- a/solution.py
+++ b/solution.py
@@ -48,8 +48,7 @@
 
 
 class Span:
-    def __init__(self, off_ref, pos_ref, seq, start, q, dtr, dtb, rate, taps):
-        first = pos_ref[0]
+    def __init__(self, off_ref, first, seq, start, q, dtr, dtb, rate, taps):
         at = first + start
         col = at + lax.broadcasted_iota(jnp.int32, (q, 1), 0)
         row = at + lax.broadcasted_iota(jnp.int32, (1, q), 1)
@@ -95,9 +94,12 @@
     return conv, shifted
 
 
-def scan_kernel(dims, off, pos, pre, rim, dtr, cw, cb, dtb, rate, dsk, y, rd, lead, st, lead0, fin, halo, state, run):
+def scan_kernel(dims, off, pos, *refs):
+    scan_chunk(dims, pl.program_id(0), pl.program_id(1), off, pos[0], *refs)
+
+
+def scan_chunk(dims, b, c, off, first, pre, rim, dtr, cw, cb, dtb, rate, dsk, y, rd, lead, st, lead0, fin, halo, state, run):
     q, inner, width, n = dims
-    b, c = pl.program_id(0), pl.program_id(1)
 
     @pl.when(c == 0)
     def _():
@@ -106,7 +108,7 @@
         run[...] = jnp.zeros_like(run)
 
     taps = cw.shape[0]
-    sp = Span(off, pos, b, c * q, q, dtr[0], dtb[...], rate[...], taps)
+    sp = Span(off, first, b, c * q, q, dtr[0], dtb[...], rate[...], taps)
     total = run[...] + sp.cum
     lead[0] = jnp.exp(total) * sp.kept_dev
     lead0[0, 0] = jnp.broadcast_to(jnp.exp(run[...]) * sp.carry_dev, (8, LANES))
@@ -154,7 +156,7 @@
     for j in range(inner // LANES):
         lo, hi = j * LANES, (j + 1) * LANES
         h = j * per
-        came = s_in[0, :, lo:hi]
+        came = s_in[0, :, lo:hi].astype(F32)
         st_full[0, 0, :, lo:hi] = st[0, 0, :, lo:hi] + widen(lead0[0, 0, 0:1], h, lane, width) * came
         val = y_in[0, :, lo:hi] + widen(lead[0], h, lane, width) * mm(rd[0], came.astype(BF16))
         y[0, :, lo:hi] = val
@@ -220,7 +222,7 @@
         carry[...] = jnp.zeros_like(carry)
 
     taps = cw.shape[0]
-    sp = Span(off, pos, b, at * q, q, dtr[0], dtb[...], rate[...], taps)
+    sp = Span(off, pos[0], b, at * q, q, dtr[0], dtb[...], rate[...], taps)
     lane = lax.broadcasted_iota(jnp.int32, (1, LANES), 1)
     per = LANES // width
 
@@ -291,6 +293,7 @@
             part = mm((fade * scores).astype(BF16), grad_low, TN)
             u = part if u is None else jnp.where(lane >= i * width, part, u)
         from_end = tail * mm(write, late_low)
+        inside = u
         u = u + from_end
         weighted = (lead * grad).astype(BF16)
         d_read = d_read + mm(weighted, early.astype(BF16), NT)
@@ -301,7 +304,11 @@
             lax.broadcasted_iota(jnp.int32, (LANES, LANES), 0) // width + h
             == lax.broadcasted_iota(jnp.int32, (LANES, LANES), 1)
         ).astype(F32)
-        d_cum = d_cum + mm(grad * core - xdt * u, head_of, precision=PRECISE)
+        d_cum = d_cum + mm(
+            grad_low.astype(F32) * core - xdt_low.astype(F32) * inside - xdt * from_end,
+            head_of,
+            precision=PRECISE,
+        )
         d_step = d_step + mm(xs * u, head_of, precision=PRECISE)
         end_row = end_lead * jnp.sum(late * early, axis=0, keepdims=True) + jnp.sum(
             xdt * from_end, axis=0, keepdims=True
@@ -518,6 +525,405 @@
     )(offs, pos, pre, pre, rim, dtr, y, dy, st, d_in, cw, cb, dtb, rate, dsk)
 
 
+MESH = pl.DeviceIdType.MESH
+
+
+def remote(src, dst, send, recv, **where):
+    return pltpu.make_async_remote_copy(
+        src_ref=src, dst_ref=dst, send_sem=send, recv_sem=recv, device_id=where, device_id_type=MESH
+    )
+
+
+class Line:
+    def __init__(self, own, full, rows, wide, send, recv):
+        self.own, self.full, self.rows, self.wide = own, full, rows, wide
+        self.send, self.recv = send, recv
+        self.me = lax.axis_index("tp")
+        self.peers = lax.axis_size("tp")
+
+    def block(self, slot):
+        return self.full.at[self.rows, pl.ds(pl.multiple_of(slot * self.wide, self.wide), self.wide)]
+
+    def parts(self, k):
+        for way, step in enumerate((1, -1)):
+            slot = self.me - k * step
+            there = self.me + step
+            held = (slot >= 0) & (slot < self.peers)
+            onward = held & (there >= 0) & (there < self.peers)
+            slot = jnp.clip(slot, 0, self.peers - 1)
+            here = self.own.at[self.rows] if k == 0 else self.block(slot)
+            copy = remote(here, self.block(slot), self.send.at[way, k], self.recv.at[slot], tp=there)
+            yield held, onward, copy
+
+    def step(self, k):
+        for held, onward, copy in self.parts(k):
+            if k > 0:
+
+                @pl.when(held)
+                def _():
+                    copy.wait_recv()
+
+            @pl.when(onward)
+            def _():
+                copy.start()
+
+    def finish(self):
+        for k in range(self.peers - 1):
+            for held, onward, copy in self.parts(k):
+
+                @pl.when(onward)
+                def _():
+                    copy.wait_send()
+
+
+def front_kernel(
+    dims, off, x, cot, wx_in, wz_in, wo_in, wbc, wdt, gain_in, cw, cb, dtb, rate, dsk, gain,
+    xn_o, r1_o, pre_o, dtr_o, z_o, y_o, rd_o, lead_o, st_o, fin_o, sq_o, part_o, rim_o, wx_o, wz_o, wo_o, cot_o,
+    x_all, xn, r1, pre, dtr, z, y, rd, lead, st, lead0, fin, sq, ygg, part, rim, rim16, came, left,
+    wx, wz, wo, halo, state, run,
+    xs_send, xs_recv, cs_send, cs_recv, w_send, w_recv, r_send, r_recv, s_send, s_recv, loc, outs,
+):
+    nb, length, q, inner, width, n, d = dims
+    tokens = nb * length
+    pair = 2 * n
+    ctx, tp, fs = lax.axis_index("ctx"), lax.axis_index("tp"), lax.axis_index("fsdp")
+    tps = lax.axis_size("tp")
+    wide = d // tps
+    deep = wx_in.shape[0]
+    mate = fs + 1 - 2 * lax.rem(fs, 2)
+    over = lax.rem(fs + 2, 4)
+    other = 1 - ctx
+    first = ctx * length
+
+    barrier = pltpu.get_barrier_semaphore()
+    pl.semaphore_signal(barrier, inc=1, device_id={"fsdp": mate}, device_id_type=MESH)
+    pl.semaphore_signal(barrier, inc=1, device_id={"fsdp": over}, device_id_type=MESH)
+    pl.semaphore_signal(barrier, inc=1, device_id={"ctx": other}, device_id_type=MESH)
+    for there in (tp - 1, tp + 1):
+
+        @pl.when((there >= 0) & (there < tps))
+        def _():
+            pl.semaphore_signal(barrier, inc=1, device_id={"tp": there}, device_id_type=MESH)
+
+    sides = (tp > 0).astype(jnp.int32) + (tp < tps - 1).astype(jnp.int32)
+    pl.semaphore_wait(barrier, 3 + sides)
+
+    def seq(m):
+        return pl.ds(m * length, length)
+
+    x_lines = [Line(x, x_all, seq(m), wide, xs_send.at[m], xs_recv.at[m]) for m in range(nb)]
+    c_lines = [Line(cot, cot_o, seq(m), wide, cs_send.at[m], cs_recv.at[m]) for m in range(nb)]
+    mine = pl.ds(pl.multiple_of(tp * wide, wide), wide)
+
+    def slot(w, at):
+        span = pl.ds(pl.multiple_of(at * deep, deep), deep)
+        return (wx.at[span], wz.at[span], wo.at[:, span])[w]
+
+    owns = (wx_in, wz_in, wo_in)
+
+    def near(w):
+        return remote(owns[w], slot(w, fs), w_send.at[w, 0], w_recv.at[w, fs], fsdp=mate)
+
+    def far(w):
+        return remote(owns[w], slot(w, fs), w_send.at[w, 1], w_recv.at[w, fs], fsdp=over)
+
+    def relay(w):
+        return remote(slot(w, over), slot(w, over), w_send.at[w, 2], w_recv.at[w, over], fsdp=mate)
+
+    def arrive(w, at):
+        remote(slot(w, at), slot(w, at), w_send.at[w, 0], w_recv.at[w, at], fsdp=mate).wait_recv()
+
+    locals_ = [pltpu.make_async_copy(owns[w], slot(w, fs), loc.at[w]) for w in range(3)]
+    locals_.append(pltpu.make_async_copy(x, x_all.at[:, mine], loc.at[3]))
+    locals_.append(pltpu.make_async_copy(cot, cot_o.at[:, mine], loc.at[4]))
+
+    x_lines[0].step(0)
+    far(0).start()
+    near(0).start()
+    for copy in locals_:
+        copy.start()
+    far(1).start()
+    near(1).start()
+    far(2).start()
+    near(2).start()
+    for k in range(1, tps):
+        x_lines[0].step(k)
+    x_lines[1].step(0)
+
+    def pass_on(w):
+        arrive(w, over)
+        relay(w).start()
+
+    def whole_weight(w):
+        arrive(w, mate)
+        arrive(w, lax.rem(mate + 2, 4))
+        locals_[w].wait()
+
+    out_copies = []
+
+    def keep(i, src, dst):
+        copy = pltpu.make_async_copy(src, dst, outs.at[i])
+        copy.start()
+        out_copies.append(copy)
+
+    def norm(m):
+        @pl.loop(0, length // q)
+        def _(i):
+            rows = pl.ds(pl.multiple_of(m * length + i * q, q), q)
+            total = jnp.zeros((q, LANES), F32)
+            for j in range(d // LANES):
+                v = x_all[rows, j * LANES : (j + 1) * LANES].astype(F32)
+                total = total + v * v
+            inv = lax.rsqrt(jnp.sum(total, axis=1, keepdims=True) * (1.0 / d) + EPSILON)
+            r1[rows, :] = jnp.broadcast_to(inv, (q, LANES))
+            for j in range(d // LANES):
+                cols = slice(j * LANES, (j + 1) * LANES)
+                xn[rows, cols] = (x_all[rows, cols].astype(F32) * inv * gain_in[:, cols]).astype(BF16)
+
+    def project_x(m):
+        tile = min(2 * LANES, inner)
+        for half in (1, 0):
+            size = length // 2
+            rows = pl.ds(m * length + half * size, size)
+            here = pl.ds(half * size, size)
+            dtr[m, here, :] = mm(xn[rows, :], wdt[...])
+            pre[m, here, inner:] = mm(xn[rows, :], wbc[...]).astype(BF16)
+
+            @pl.loop(0, inner // tile)
+            def _(j):
+                cols = pl.ds(pl.multiple_of(j * tile, tile), tile)
+                pre[m, here, cols] = mm(xn[rows, :], wx[:, cols]).astype(BF16)
+
+            if half == 1:
+
+                @pl.when(ctx == 0)
+                def _():
+                    rim_copy(m).start()
+
+    def rim_copy(m):
+        return remote(pre.at[m, pl.ds(length - 16, 16)], rim16.at[m], r_send.at[m], r_recv.at[m], ctx=other)
+
+    def project_z(m):
+        tile = min(2 * LANES, inner)
+        rows = seq(m)
+
+        @pl.loop(0, inner // tile)
+        def _(j):
+            cols = pl.ds(pl.multiple_of(j * tile, tile), tile)
+            z[m, :, cols] = mm(xn[rows, :], wz[:, cols])
+
+    def one(ref, m):
+        return ref.at[pl.ds(m, 1)]
+
+    def span(ref, m, rows):
+        return ref.at[pl.ds(m, 1), rows]
+
+    def get_rim(m):
+        @pl.when(ctx == 1)
+        def _():
+            rim_copy(m).wait_recv()
+            rim[m] = rim16[m, 8:16].astype(F32)
+
+        @pl.when(ctx == 0)
+        def _():
+            rim[m] = jnp.zeros_like(rim[m])
+
+    def scan(m, lo, hi):
+        @pl.loop(lo, hi)
+        def _(c):
+            rows = pl.ds(pl.multiple_of(c * q, q), q)
+            scan_chunk(
+                (q, inner, width, n), m, c, off, first,
+                span(pre, m, rows), one(rim, m), span(dtr, m, rows), cw, cb, dtb, rate, dsk,
+                span(y, m, rows), span(rd, m, rows), span(lead, m, rows),
+                st.at[pl.ds(m, 1), pl.ds(c, 1)], lead0.at[pl.ds(m, 1), pl.ds(c, 1)], one(fin, m),
+                halo, state, run,
+            )
+
+    def state_copy(m):
+        return remote(left.at[m], came.at[m], s_send.at[m], s_recv.at[m], ctx=other)
+
+    def send_state(m):
+        @pl.when(ctx == 0)
+        def _():
+            left[m] = fin[m].astype(BF16)
+            state_copy(m).start()
+
+    def get_state(m):
+        @pl.when(ctx == 1)
+        def _():
+            state_copy(m).wait_recv()
+
+        @pl.when(ctx == 0)
+        def _():
+            came[m] = jnp.zeros_like(came[m])
+
+    def gate(m):
+        @pl.loop(0, length // q)
+        def _(c):
+            rows = pl.ds(pl.multiple_of(c * q, q), q)
+            sts = st.at[pl.ds(m, 1), pl.ds(c, 1)]
+            ys = span(y, m, rows)
+            gate_kernel(
+                (q, inner, width, n), ys, span(rd, m, rows), span(lead, m, rows),
+                lead0.at[pl.ds(m, 1), pl.ds(c, 1)], sts, one(came, m), span(z, m, rows), gain,
+                ys, span(ygg, m, rows), span(sq, m, rows), sts,
+            )
+
+    def project_out(m):
+        tile = 2 * LANES
+
+        @pl.loop(0, d // tile)
+        def _(j):
+            cols = pl.ds(pl.multiple_of(j * tile, tile), tile)
+            part[seq(m), cols] = mm(ygg[m], wo[:, cols]).astype(BF16)
+
+    locals_[3].wait()
+    pass_on(0)
+    norm(0)
+    whole_weight(0)
+    keep(0, wx, wx_o)
+    project_x(0)
+    x_lines[1].step(1)
+    pass_on(1)
+    get_rim(0)
+    scan(0, 0, length // q)
+    send_state(0)
+    x_lines[1].step(2)
+    whole_weight(1)
+    keep(1, wz, wz_o)
+    project_z(0)
+    for k in range(3, tps):
+        x_lines[1].step(k)
+    pass_on(2)
+    c_lines[0].step(0)
+    norm(1)
+    project_x(1)
+    keep(2, xn, xn_o)
+    keep(3, r1, r1_o)
+    keep(4, pre, pre_o)
+    keep(5, dtr, dtr_o)
+    c_lines[0].step(1)
+    get_rim(1)
+    keep(6, rim, rim_o)
+    scan(1, 0, length // q)
+    send_state(1)
+    keep(7, rd, rd_o)
+    keep(8, lead, lead_o)
+    keep(9, fin, fin_o)
+    c_lines[0].step(2)
+    project_z(1)
+    keep(10, z, z_o)
+    get_state(0)
+    gate(0)
+    for k in range(3, tps):
+        c_lines[0].step(k)
+    c_lines[1].step(0)
+    whole_weight(2)
+    keep(11, wo, wo_o)
+    project_out(0)
+    get_state(1)
+    c_lines[1].step(1)
+    gate(1)
+    keep(12, y, y_o)
+    keep(13, st, st_o)
+    keep(14, sq, sq_o)
+    project_out(1)
+    keep(15, part, part_o)
+    for k in range(2, tps):
+        c_lines[1].step(k)
+    for line in x_lines + c_lines:
+        line.finish()
+    for w in range(3):
+        near(w).wait_send()
+        far(w).wait_send()
+        relay(w).wait_send()
+    locals_[4].wait()
+
+    @pl.when(ctx == 0)
+    def _():
+        for m in range(nb):
+            rim_copy(m).wait_send()
+            state_copy(m).wait_send()
+
+    for copy in out_copies:
+        copy.wait()
+
+
+def front(offs, x, cot, wx, wz, wo, wbc, wdt, gain_in, cw, cb, dtb, rate, dsk, gain, nb, length, width, n, tps):
+    tokens, wide = x.shape
+    d = wide * tps
+    inner = wx.shape[1]
+    chans = cw.shape[1]
+    q = min(CHUNK, length)
+    chunks = length // q
+    dims = (nb, length, q, inner, width, n, d)
+    sds = jax.ShapeDtypeStruct
+    kept = [
+        sds((tokens, d), BF16),
+        sds((tokens, LANES), F32),
+        sds((nb, length, chans), BF16),
+        sds((nb, length, LANES), F32),
+        sds((nb, length, inner), F32),
+        sds((nb, length, inner), F32),
+        sds((nb, length, n), BF16),
+        sds((nb, length, LANES), F32),
+        sds((nb, chunks, n, inner), F32),
+        sds((nb, n, inner), F32),
+        sds((nb, length, LANES), F32),
+        sds((tokens, d), BF16),
+        sds((nb, 8, chans), F32),
+        sds((d, inner), BF16),
+        sds((d, inner), BF16),
+        sds((inner, d), BF16),
+        sds((tokens, d), BF16),
+    ]
+
+    def vm(k):
+        return pltpu.VMEM(kept[k].shape, kept[k].dtype)
+
+    scratch = [
+        pltpu.VMEM((tokens, d), BF16),
+        vm(0), vm(1), vm(2), vm(3), vm(4), vm(5), vm(6), vm(7), vm(8),
+        pltpu.VMEM((nb, chunks, 8, LANES), F32),
+        vm(9), vm(10),
+        pltpu.VMEM((nb, length, inner), BF16),
+        vm(11), vm(12),
+        pltpu.VMEM((nb, 16, chans), BF16),
+        pltpu.VMEM((nb, n, inner), BF16),
+        pltpu.VMEM((nb, n, inner), BF16),
+        vm(13), vm(14), vm(15),
+        pltpu.VMEM((8, chans), F32),
+        pltpu.VMEM((n, inner), F32),
+        pltpu.VMEM((1, LANES), F32),
+        pltpu.SemaphoreType.DMA((nb, 2, tps)),
+        pltpu.SemaphoreType.DMA((nb, tps)),
+        pltpu.SemaphoreType.DMA((nb, 2, tps)),
+        pltpu.SemaphoreType.DMA((nb, tps)),
+        pltpu.SemaphoreType.DMA((3, 3)),
+        pltpu.SemaphoreType.DMA((3, 4)),
+        pltpu.SemaphoreType.DMA((nb,)),
+        pltpu.SemaphoreType.DMA((nb,)),
+        pltpu.SemaphoreType.DMA((nb,)),
+        pltpu.SemaphoreType.DMA((nb,)),
+        pltpu.SemaphoreType.DMA((5,)),
+        pltpu.SemaphoreType.DMA((16,)),
+    ]
+    hbm = pl.BlockSpec(memory_space=pl.ANY)
+    vmem = pl.BlockSpec(memory_space=pltpu.VMEM)
+    return pl.pallas_call(
+        functools.partial(front_kernel, dims),
+        in_specs=[pl.BlockSpec(memory_space=pltpu.SMEM)] + [hbm] * 5 + [vmem] * 9,
+        out_specs=[hbm] * len(kept),
+        out_shape=kept,
+        scratch_shapes=scratch,
+        compiler_params=pltpu.CompilerParams(
+            collective_id=0, has_side_effects=True, vmem_limit_bytes=60 << 20
+        ),
+        name="front",
+    )(offs, x, cot, wx, wz, wo, wbc, wdt, gain_in, cw, cb, dtb, rate, dsk, gain)
+
+
 def shift(arr, axis, by):
     peers = lax.axis_size(axis)
     pairs = [(i, i + by) for i in range(peers) if 0 <= i + by < peers]
@@ -575,39 +981,49 @@
 
     x_own = x_in.reshape(tokens, width_dev)
     cot_own = cotangent.reshape(tokens, width_dev)
-    x_all = lax.all_gather(x_own, "tp", axis=1, tiled=True)
+    tps = lax.axis_size("tp")
     small = jnp.concatenate([w_bc, w_dt], axis=1)
     small = lax.all_gather(small, "fsdp", axis=0, tiled=True)
-    wdt = jnp.pad(small[:, pair // lax.axis_size("tp") :], ((0, 0), (0, LANES - heads)))
-    wbc = lax.all_gather(small[:, : pair // lax.axis_size("tp")], "tp", axis=1, tiled=True)
-    wx = lax.all_gather(w_x, "fsdp", axis=0, tiled=True)
-    wz = lax.all_gather(w_z, "fsdp", axis=0, tiled=True)
-    wo = lax.all_gather(w_out, "fsdp", axis=1, tiled=True)
-    cot_all = lax.all_gather(cot_own, "tp", axis=1, tiled=True)
-    wxbc = jnp.concatenate([wx, wbc], axis=1)
-
-    resid = x_all.astype(F32)
-    r1 = lax.rsqrt(jnp.mean(resid * resid, axis=1, keepdims=True) + EPSILON)
-    xn = (resid * r1 * in_gain).astype(BF16)
-    pre = mm(xn, wxbc).astype(BF16).reshape(nb, length, inner + pair)
-    dtr = mm(xn, wdt).reshape(nb, length, LANES)
-    z = mm(xn, wz).reshape(nb, length, inner)
-    rim = shift(pre[:, length - 8 :], "ctx", 1).astype(F32)
-    y, rd, lead, st, lead0, fin = scan_forward(
-        offs, pos, pre, rim, dtr, cw, cb, dtb, rate, dsk, width, n
-    )
-    lend = jnp.repeat(lead[:, length - 1, :heads], width, axis=-1)[:, None]
-
-    def chained(start, by):
+    wdt = jnp.pad(small[:, pair // tps :], ((0, 0), (0, LANES - heads)))
+    wbc = lax.all_gather(small[:, : pair // tps], "tp", axis=1, tiled=True)
+
+    def chained(start, lend, by):
         came = jnp.zeros_like(start)
         for k in range(peers - 1):
             sent = start if k == 0 else start + lend * came
             came = shift(sent.astype(BF16), "ctx", by).astype(F32)
         return came
 
-    s_in = chained(fin, 1)
-    y, ygg, sq, st = gate_forward(y, rd, lead, lead0, st, s_in, z, gain, width)
-    part = mm(ygg.reshape(tokens, inner), wo).astype(BF16)
+    def ending(lead):
+        return jnp.repeat(lead[:, length - 1, :heads], width, axis=-1)[:, None]
+
+    if peers == 2 and lax.axis_size("fsdp") == 4:
+        xn, r1, pre, dtr, z, y, rd, lead, st, _, sq, part, rim, wx, wz, wo, cot_all = front(
+            offs, x_own, cot_own, w_x, w_z, w_out, wbc, wdt, in_gain[None], cw, cb, dtb, rate, dsk, gain,
+            nb, length, width, n, tps,
+        )
+        r1 = r1[:, :1]
+    else:
+        x_all = lax.all_gather(x_own, "tp", axis=1, tiled=True)
+        wx = lax.all_gather(w_x, "fsdp", axis=0, tiled=True)
+        wz = lax.all_gather(w_z, "fsdp", axis=0, tiled=True)
+        wo = lax.all_gather(w_out, "fsdp", axis=1, tiled=True)
+        cot_all = lax.all_gather(cot_own, "tp", axis=1, tiled=True)
+        resid = x_all.astype(F32)
+        r1 = lax.rsqrt(jnp.mean(resid * resid, axis=1, keepdims=True) + EPSILON)
+        xn = (resid * r1 * in_gain).astype(BF16)
+        pre = jnp.concatenate([mm(xn, wx).astype(BF16), mm(xn, wbc).astype(BF16)], axis=1)
+        pre = pre.reshape(nb, length, inner + pair)
+        dtr = mm(xn, wdt).reshape(nb, length, LANES)
+        z = mm(xn, wz).reshape(nb, length, inner)
+        rim = shift(pre[:, length - 8 :], "ctx", 1).astype(F32)
+        y, rd, lead, st, lead0, fin = scan_forward(
+            offs, pos, pre, rim, dtr, cw, cb, dtb, rate, dsk, width, n
+        )
+        s_in = chained(fin, ending(lead), 1)
+        y, ygg, sq, st = gate_forward(y, rd, lead, lead0, st, s_in, z, gain, width)
+        part = mm(ygg.reshape(tokens, inner), wo).astype(BF16)
+    lend = ending(lead)
     share = lax.psum_scatter(part, "tp", scatter_dimension=1, tiled=True)
     dyn = mm(cot_all, wo, NT).reshape(nb, length, inner)
     dot = jnp.sum(dyn * gain * y * jax.nn.silu(z), axis=2)
@@ -619,7 +1035,7 @@
     dy, dz, yn, g_gain, g_state = gate_backward(dyn, y, z, stat, gain, rd, lead, width, inner_all)
     dz = dz.reshape(tokens, inner)
     yn = yn.reshape(tokens, inner)
-    d_in = chained(g_state, -1)
+    d_in = chained(g_state, lend, -1)
     rows = ("ctx", "fsdp")
 
     def scattered(grad):
@@ -633,7 +1049,7 @@
     edge = (edge + shift(rim_grad, "ctx", -1)).astype(BF16)
     dcat = lax.dynamic_update_slice(dcat, edge, (0, length - 8, 0)).reshape(tokens, inner + pair)
     ddt = ddt.reshape(tokens, LANES)
-    dxn = mm(dz, wz, NT) + mm(dcat, wxbc, NT) + mm(ddt, wdt, NT)
+    dxn = mm(dz, wz, NT) + mm(dcat[:, :inner], wx, NT) + mm(dcat[:, inner:], wbc, NT) + mm(ddt, wdt, NT)
     dxn = lax.psum_scatter(dxn.astype(BF16), "tp", scatter_dimension=1, tiled=True).astype(F32)
     g_xbc = scattered(jnp.concatenate([mm(xn, dcat, TN), mm(xn, ddt, TN)[:, :heads]], axis=1))
     g_x = g_xbc[:, :inner].astype(F32)

time: 909 us -> 783 us (0.86)
  waiting for transfers between devices: 615 us -> 393 us
  Pallas kernels: 95 us -> 208 us
  matrix products: 81.7 us -> 59.7 us
  local copies, waits for them, and re-layouts: 18.8 us -> 34.8 us
    all_gather x6 -> x1, waiting for transfers between devices: 243 us -> 20.6 us  [on_device(): wbc = lax.all_gather(small[:, :pair // tps], 'tp', axis=1, tiled=True)]
    pallas_call x2 -> x1, Pallas kernels: 29.8 us -> 143 us  [front(): pl.pallas_call(functools.partial(front_kernel, dims), in_specs=[pl.BlockS...]
    dot_general x12 -> x9, matrix products: 81.7 us -> 59.7 us  [mm(): lax.dot_general(a, b, (dims, ((), ())), precision=precision, preferred_el...]
    unnamed x16 -> x11, waiting for transfers between devices: 89 us -> 87.2 us
  transfers between devices with their start and end apart: 18 -> 11, of which waited for: 15 -> 10; matrix products, arithmetic and copies ran while one was open for 12% -> 10% of each run, Pallas kernels for 2% -> 0%
where the time goes in v2:
time: 783 us; the launch traced here: 774 us
  waiting for transfers between devices  393 us (50%)
  Pallas kernels  208 us (27%)
  matrix products  59.7 us (8%)
  blocking collectives  35.3 us (5%)
  local copies, waits for them, and re-layouts  34.8 us (4%)
  other arithmetic  23.2 us (3%)
  between operations  16.3 us (2%)
    reduce_scatter x3, waiting for transfers between devices, scattered(): lax.psum_scatter(grad.astype(BF16), rows, scatter_dimension=0, tiled=True)  159 us
    pallas_call x1, Pallas kernels, front(): pl.pallas_call(functools.partial(front_kernel, dims), in_specs=[pl.BlockS...  143 us
    unnamed x11, waiting for transfers between devices  87.2 us
    dot_general x9, matrix products, mm(): lax.dot_general(a, b, (dims, ((), ())), precision=precision, preferred_el...  59.7 us
    reduce_scatter x1, waiting for transfers between devices, on_device(): share = lax.psum_scatter(part, 'tp', scatter_dimension=1, tiled=True)  59.6 us
    pallas_call x1, Pallas kernels, scan_backward(): pl.pallas_call(functools.partial(back_kernel, dims), grid_spec=pltpu.Pref...  54.7 us
    reduce_scatter x1, waiting for transfers between devices, on_device(): lax.psum_scatter(dxn.astype(BF16), 'tp', scatter_dimension=1, tiled=True)  40.3 us
    all_gather x1, waiting for transfers between devices, on_device(): wbc = lax.all_gather(small[:, :pair // tps], 'tp', axis=1, tiled=True)  20.6 us
  transfers between devices with their start and end apart: 11, of which 10 were waited for; matrix products, arithmetic and copies ran while one was open for 10% of the time, Pallas kernels for 0%

profile of v2, /device:TPU:0, one launch (start us, length us, event | category | flops | bytes accessed | tf_op | source)
XLA Modules:
  0.0 773.8 jit_solution(1832734870392849883)
XLA Ops:
  8.1 1.0 copy.66
  9.2 8.6 %all_gather.30 = bf16[2048,80]{1,0:T(8,128)(2,1)S(1)} all-gather(bf16[512,80]{1,0:T(8,128)(2,1)S(1)} %pad_maximum_fusion.1), channel_id=1, replica_groups=mesh['ctx'=2,'tp'=4,'fsdp'=4] {'fsdp'}, dimensions={0}, use_global_device_ids=true | all-gather | bytes 409600 | tf_op jit(solution)/shard_map/all_gather | solution.py:986
  17.8 0.9 copy.68
  24.3 1.3 dynamic_slice.26
  27.1 20.6 %all-gather.6.cloned.1.call-done = bf16[2048,256]{0,1:T(8,128)(2,1)} async-done(((bf16[2048,64]{0,1:T(8,128)(2,1)}), bf16[2048,256]{0,1:T(8,128)(2,1)}) %all-gather.6.cloned.1.call-update) | async-done | bytes 1048592 | tf_op jit(solution)/shard_map/all_gather | solution.py:988
  47.7 2.3 copy.69.wbc
  49.9 142.9 %front.1 = (bf16[1024,2048]{1,0:T(8,128)(2,1)}, f32[1024,128]{1,0:T(8,128)}, bf16[2,512,1280]{2,1,0:T(8,128)(2,1)}, f32[2,512,128]{2,1,0:T(8,128)}, f32[2,512,10...) custom-call(s32[2,4]{1,0:T(2,128)} %bitcast.96, ...), custom_call_target="tpu_custom_call" | custom-call | tf_op jit(solution)/shard_map/front/pallas_call | solution.py:914
  192.9 1.3 slice_reduce_fusion
  194.2 7.7 fusion.21
  202.0 1.3 multiply_reduce_fusion
  203.9 13.1 %all-gather = f32[8,2,512]{2,1,0:T(2,128)S(1)} all-gather(f32[2,2,512]{2,1,0:T(2,128)S(1)} %pad_maximum_fusion.6), channel_id=2, replica_groups=mesh['ctx'=2,'tp'=4,'fsdp'=4] {'tp'}, dimensions={0}, use_global_device_ids=true | all-gather | bytes 40960 | tf_op jit(solution)/shard_map/all_gather | solution.py:1031
  217.8 10.8 %gate_backward.1 = (f32[2,512,1024]{2,1,0:T(8,128)}, bf16[2,512,1024]{2,1,0:T(8,128)(2,1)S(1)}, bf16[2,512,1024]{2,1,0:T(8,128)(2,1)}, f32[8,1024]{1,0:T(8,128)S(1)}, f32[2,128,1024]{2,1,0:T(8,128)S(1)}) custom-call(f32[2,512,1024]{2,1,0:T(8,128)} %bitcast.101, f32[2,512,1024]{2,1,0:T(8,128)} %get-tuple-element.44.y, f32[2,512,1024]{2,1,0:T(8,128)} %get-tuple-element.45.z, ...), custom_call_target="tpu_custom_call" | custom-call | tf_op jit(solution)/shard_map/gate_backward/pallas_call | solution.py:438
  228.7 1.3 copy-done.13
  230.1 1.3 collective-permute-start
  231.4 9.8 %collective-permute-done = bf16[2,128,1024]{2,1,0:T(8,128)(2,1)S(1)} collective-permute-done((bf16[2,128,1024]{2,1,0:T(8,128)(2,1)S(1)}, bf16[2,128,1024]{2,1,0:T(8,128)(2,1)S(1)}, u32[]{:S(2)}, u32[]{:S(2)}) %collective-permute-start) | collective-permute-done | bytes 524320 | tf_op jit(solution)/shard_map/ppermute | solution.py:930
  241.4 54.7 %scan_backward.1 = (bf16[2,512,1280]{2,1,0:T(8,128)(2,1)S(1)}, bf16[2,512,128]{2,1,0:T(8,128)(2,1)S(1)}, f32[2,8,1280]{2,1,0:T(8,128)S(1)}, f32[2,8,1280]{2,1,0:...) custom-call(s32[2,4]{1,0:T(2,128)S(1)} %bitcast.97, s32[1]{0:T(128)} %bitcast.15.pos, ...), custom_call_target="tpu_custom_call" | custom-call | tf_op jit(solution)/shard_map/scan_backward/pallas_call | solution.py:483
  296.1 1.5 collective-permute-start.1
  297.6 9.0 %fusion.22 = f32[1024,2048]{1,0:T(8,128)} fusion(bf16[1024,1024]{1,0:T(8,128)(2,1)S(1)} %bitcast.98, bf16[2048,1024]{1,0:T(8,128)(2,1)} %get-tuple-element.51), kind=kOutput, calls=%fused_computation.68 | convolution fusion | flops 4294967296 | bytes 14680064 | tf_op jit(solution)/shard_map/dot_general | solution.py:20
  306.7 6.9 fusion.8
  313.6 1.3 fusion.11
  314.8 9.0 %add_convert_fusion = bf16[1024,2048]{1,0:T(8,128)(2,1)} fusion(f32[1024,2048]{1,0:T(8,128)S(1)} %fusion.11, f32[1024,2048]{1,0:T(8,128)} %fusion.22, f32[1024,2048]{1,0:T(8,128)} %fusion.8, bf16[1024,128]{1,0:T(8,128)(2,1)S(1)} %bitcast.89, bf16[2048,16]{1,0:T(8,128)(2,1)S(1)} %slice.126), kind=kOutput, calls=%fused_computation | convolution fusion | flops 545259520 | bytes 29687808 | tf_op jit(solution)/shard_map/dot_general | solution.py:20
  323.9 1.5 copy-done.29
  325.4 8.3 %convolution_convert_fusion.1 = bf16[2048,1024]{1,0:T(8,128)(2,1)} fusion(bf16[1024,2048]{1,0:T(8,128)(2,1)} %get-tuple-element.42, bf16[1024,1024]{1,0:T(8,128)(2,1)S(1)} %bitcast.122), kind=kOutput, calls=%fused_computation.4 | convolution fusion | flops 4297064448 | bytes 10485760 | tf_op jit(solution)/shard_map/dot_general | solution.py:20
  333.9 1.5 copy-done.15
  335.4 8.3 %convolution_convert_fusion.2 = bf16[2048,1024]{1,0:T(8,128)(2,1)} fusion(bf16[1024,2048]{1,0:T(8,128)(2,1)} %get-tuple-element.66, bf16[1024,1024]{1,0:T(8,128)(2,1)S(1)} %bitcast.99), kind=kOutput, calls=%fused_computation.5 | convolution fusion | flops 4297064448 | bytes 10485760 | tf_op jit(solution)/shard_map/dot_general | solution.py:20
  344.0 3.2 fusion.23
  348.1 5.9 convolution_convert_fusion
  354.0 2.9 pad_maximum_fusion
  359.7 40.3 %reduce-scatter.9.cloned.1.call-done = bf16[1024,512]{1,0:T(8,128)(2,1)} async-done(((bf16[1024,2048]{1,0:T(8,128)(2,1)}), bf16[1024,512]{1,0:T(8,128)(2,1)}) %reduce-scatter.9.cloned.1.call-update) | async-done | bytes 1048592 | tf_op jit(solution)/shard_map/reduce_scatter | solution.py:1053
  400.0 2.2 fusion.7
  405.7 50.0 %reduce-scatter.17.cloned.1.call-done = bf16[256,1024]{1,0:T(8,128)(2,1)} async-done(((bf16[2048,1024]{1,0:T(8,128)(2,1)}), bf16[256,1024]{1,0:T(8,128)(2,1)}) %reduce-scatter.17.cloned.1.call-update) | async-done | bytes 524304 | tf_op jit(solution)/shard_map/reduce_scatter | solution.py:1042
  455.7 2.1 convert_bitcast_fusion
  457.8 2.7 copy.76
  460.5 49.7 %reduce-scatter.11.cloned.1.call-done = bf16[256,1024]{1,0:T(8,128)(2,1)} async-done(((bf16[2048,1024]{1,0:T(8,128)(2,1)}), bf16[256,1024]{1,0:T(8,128)(2,1)}) %reduce-scatter.11.cloned.1.call-update) | async-done | bytes 524304 | tf_op jit(solution)/shard_map/reduce_scatter | solution.py:1042
  510.2 2.1 convert_element_type.61
  512.3 58.9 %reduce-scatter.13.cloned.1.call-done = bf16[256,1296]{0,1:T(8,128)(2,1)} async-done(((bf16[2048,1296]{0,1:T(8,128)(2,1)}), bf16[256,1296]{0,1:T(8,128)(2,1)}) %reduce-scatter.13.cloned.1.call-update) | async-done | bytes 663568 | tf_op jit(solution)/shard_map/reduce_scatter | solution.py:1042
  571.3 2.1 slice_convert_fusion
  573.4 2.5 copy.75
  575.9 52.7 %all-reduce.9.cloned.1.call-done = f32[63872]{0:T(1024)} async-done(((f32[63872]{0:T(1024)}), f32[63872]{0:T(1024)}) %all-reduce.9.cloned.1.call-update) | async-done | bytes 255504
  628.6 1.1 reshape.151
  631.1 1.6 slice_convert_fusion.1
  632.8 1.3 slice_convert_fusion.3
  634.1 13.5 %all-gather.1 = f32[4096]{0:T(1024)S(1)} all-gather(f32[1024]{0:T(1024)S(1)} %get-tuple-element.139), channel_id=3, replica_groups=mesh['ctx'=2,'tp'=4,'fsdp'=4] {'tp'}, dimensions={0}, use_global_device_ids=true | all-gather | bytes 20480 | tf_op jit(solution)/shard_map/all_gather | solution.py:1062
  647.6 59.6 %reduce-scatter.7.cloned.1.call-done = bf16[1024,512]{1,0:T(8,128)(2,1)} async-done(((bf16[1024,2048]{1,0:T(8,128)(2,1)}), bf16[1024,512]{1,0:T(8,128)(2,1)}) %reduce-scatter.7.cloned.1.call-update) | async-done | bytes 1048592 | tf_op jit(solution)/shard_map/reduce_scatter | solution.py:1027
  707.3 3.7 fusion.2
  710.9 33.7 %all-reduce.11.cloned.1.call-done = f32[31936]{0:T(1024)} async-done(((f32[31936]{0:T(1024)}), f32[31936]{0:T(1024)}) %all-reduce.11.cloned.1.call-update) | async-done | bytes 127760
  744.7 1.0 reshape.152
  750.3 16.5 %reduce-scatter.15.cloned.1.call-done = f32[256,64]{0,1:T(8,128)} async-done(((f32[256,256]{0,1:T(8,128)}), f32[256,64]{0,1:T(8,128)}) %reduce-scatter.15.cloned.1.call-update) | async-done | bytes 65552 | tf_op jit(solution)/shard_map/reduce_scatter | solution.py:1057
  (146 shorter events, 21.7 us)
Async XLA Ops:
  7.2 19.3 %copy-start.26 = (f32[4,4352]{1,0:T(4,128)S(1)}, f32[4,4352]{1,0:T(4,128)}, u32[]{:S(2)}) copy-start(f32[4,4352]{1,0:T(4,128)} %param.23) | copy-start | bytes 208900
  7.2 19.3 %slice-start = ((f32[4,4352]{1,0:T(4,128)}), f32[4,256]{1,0:T(4,128)S(1)}, s32[]{:S(2)}) async-start(f32[4,4352]{1,0:T(4,128)} %param.23), calls=%async_computation.15 | async-start | bytes 8192 | tf_op jit(solution)/shard_map/slice | solution.py:972
  7.2 40.5 %all-gather.6.cloned.1.call-start = ((), (), s32[]{:S(2)}) async-start(), calls=%async_computation.6 | async-start | bytes 1310720 | tf_op jit(solution)/shard_map/all_gather | solution.py:988
  18.7 381.3 %reduce-scatter.9.cloned.1.call-start = ((), (), s32[]{:S(2)}) async-start(), calls=%async_computation.8 | async-start | bytes 5242880 | tf_op jit(solution)/shard_map/reduce_scatter | solution.py:1053
  194.1 7.8 %copy-start.7 = (f32[1024]{0:T(1024)S(1)}, f32[1024]{0:T(1024)}, u32[]{:S(2)}) copy-start(f32[1024]{0:T(1024)} %dynamic_slice.26) | copy-start | bytes 12292
  194.1 7.8 %copy-start.16 = (f32[2,512,1024]{2,1,0:T(8,128)S(1)}, f32[2,512,1024]{2,1,0:T(8,128)}, u32[]{:S(2)}) copy-start(f32[2,512,1024]{2,1,0:T(8,128)} %get-tuple-element.44.y) | copy-start | bytes 12582916
  194.2 7.8 %copy-start.17 = (f32[2,512,1024]{2,1,0:T(8,128)S(1)}, f32[2,512,1024]{2,1,0:T(8,128)}, u32[]{:S(2)}) copy-start(f32[2,512,1024]{2,1,0:T(8,128)} %get-tuple-element.45.z) | copy-start | bytes 12582916
  201.9 2.0 copy-start.18
  202.0 15.8 %copy-start.1 = (f32[2,512,128]{2,1,0:T(8,128)S(1)}, f32[2,512,128]{2,1,0:T(8,128)}, u32[]{:S(2)}) copy-start(f32[2,512,128]{2,1,0:T(8,128)} %get-tuple-element.49.lead) | copy-start | bytes 1572868
  202.0 15.8 %copy-start.2 = (bf16[2,512,128]{2,1,0:T(8,128)(2,1)S(1)}, bf16[2,512,128]{2,1,0:T(8,128)(2,1)}, u32[]{:S(2)}) copy-start(bf16[2,512,128]{2,1,0:T(8,128)(2,1)} %get-tuple-element.48.rd) | copy-start | bytes 786436
  217.8 23.5 %copy-start = (f32[2,512,128]{2,1,0:T(8,128)S(1)}, f32[2,512,128]{2,1,0:T(8,128)}, u32[]{:S(2)}) copy-start(f32[2,512,128]{2,1,0:T(8,128)} %get-tuple-element.54.dtr) | copy-start | bytes 1572868
  217.8 23.5 %copy-start.3 = (f32[4,1280]{1,0:T(4,128)S(1)}, f32[4,1280]{1,0:T(4,128)}, u32[]{:S(2)}) copy-start(f32[4,1280]{1,0:T(4,128)} %pad_maximum_fusion.3.cw) | copy-start | bytes 61444
  217.8 23.5 %copy-start.6 = (f32[2,8,1280]{2,1,0:T(8,128)S(1)}, f32[2,8,1280]{2,1,0:T(8,128)}, u32[]{:S(2)}) copy-start(f32[2,8,1280]{2,1,0:T(8,128)} %get-tuple-element.53.rim) | copy-start | bytes 245764
  217.8 23.5 %copy-start.8 = (f32[1,1280]{1,0:T(1,128)S(1)}, f32[1,1280]{1,0:T(1,128)}, u32[]{:S(2)}) copy-start(f32[1,1280]{1,0:T(1,128)} %broadcast_in_dim.24.cb) | copy-start | bytes 15364
  217.8 23.5 %copy-start.9 = (f32[1,1024]{1,0:T(1,128)S(1)}, f32[1,1024]{1,0:T(1,128)}, u32[]{:S(2)}) copy-start(f32[1,1024]{1,0:T(1,128)} %broadcast_in_dim_reshape.3.dsk) | copy-start | bytes 12292
  217.8 23.5 %copy-start.10 = (s32[2,1,4]{2,1,0:T(1,128)S(1)}, s32[2,1,4]{2,1,0:T(1,128)}, u32[]{:S(2)}) copy-start(s32[2,1,4]{2,1,0:T(1,128)} %param.17) | copy-start | bytes 100
  217.8 23.5 %copy-start.11 = (f32[1,128]{1,0:T(1,128)S(1)}, f32[1,128]{1,0:T(1,128)}, u32[]{:S(2)}) copy-start(f32[1,128]{1,0:T(1,128)} %pad.17.rate) | copy-start | bytes 1540
  217.8 23.5 %copy-start.12 = (f32[1,128]{1,0:T(1,128)S(1)}, f32[1,128]{1,0:T(1,128)}, u32[]{:S(2)}) copy-start(f32[1,128]{1,0:T(1,128)} %pad.16.dtb) | copy-start | bytes 1540
  228.7 1.3 copy-start.13
  230.1 11.1 %collective-permute-start = (bf16[2,128,1024]{2,1,0:T(8,128)(2,1)S(1)}, bf16[2,128,1024]{2,1,0:T(8,128)(2,1)S(1)}, u32[]{:S(2)}, u32[]{:S(2)}) collective-permute-start(bf16[2,128,1024]{2,1,0:T(8,128)(2,1)S(1)} %convert_element_type.55), channel_id=1, source_target_pairs={{16,0},{17,1},{18,2},{19,3},{20,4},{21,5},{22,6},{23,7},{24,8},{25... | collective-permute-start | bytes 1572872 | tf_op jit(solution)/shard_map/ppermute | solution.py:930
  241.3 56.2 %copy-start.14 = (bf16[2,512,1024]{2,1,0:T(8,128)(2,1)S(1)}, bf16[2,512,1024]{2,1,0:T(8,128)(2,1)}, u32[]{:S(2)}) copy-start(bf16[2,512,1024]{2,1,0:T(8,128)(2,1)} %copy-done.13) | copy-start | bytes 6291460
  296.1 10.6 %collective-permute-start.1 = (f32[2,8,1280]{2,1,0:T(8,128)S(1)}, f32[2,8,1280]{2,1,0:T(8,128)S(1)}, u32[]{:S(2)}, u32[]{:S(2)}) collective-permute-start(f32[2,8,1280]{2,1,0:T(8,128)S(1)} %get-tuple-element.60), channel_id=1, source_target_pairs={{16,0},{17,1},{18,2},{19,3},{20,4},{21,5},{22,6},{23,7},{24,8},{25... | collective-permute-start | bytes 245768 | tf_op jit(solution)/shard_map/ppermute | solution.py:930
  297.6 9.1 %copy-start.28 = (bf16[2048,1024]{1,0:T(8,128)(2,1)S(1)}, bf16[2048,1024]{1,0:T(8,128)(2,1)}, u32[]{:S(2)}) copy-start(bf16[2048,1024]{1,0:T(8,128)(2,1)} %get-tuple-element.61) | copy-start | bytes 12582916
  306.7 6.9 copy-start.4
  306.7 6.9 copy-start.21
  323.9 1.6 copy-start.29
  323.9 131.8 %reduce-scatter.17.cloned.1.call-start = ((), (), s32[]{:S(2)}) async-start(), calls=%async_computation.12 | async-start | bytes 4718592 | tf_op jit(solution)/shard_map/reduce_scatter | solution.py:1042
  333.8 1.6 copy-start.15
  333.8 176.4 %reduce-scatter.11.cloned.1.call-start = ((), (), s32[]{:S(2)}) async-start(), calls=%async_computation.9 | async-start | bytes 4718592 | tf_op jit(solution)/shard_map/reduce_scatter | solution.py:1042
  343.7 3.5 copy-start.5
  343.7 227.6 %reduce-scatter.13.cloned.1.call-start = ((), (), s32[]{:S(2)}) async-start(), calls=%async_computation.10 | async-start | bytes 5971968 | tf_op jit(solution)/shard_map/reduce_scatter | solution.py:1042
  344.0 4.0 copy-start.27
  356.9 1.0 copy-start.31
  356.9 2.2 copy-start.24
  356.9 43.2 %copy-start.19 = (bf16[2,1,512,512]{3,2,1,0:T(8,128)(2,1)S(1)}, bf16[2,1,512,512]{3,2,1,0:T(8,128)(2,1)}, u32[]{:S(2)}) copy-start(bf16[2,1,512,512]{3,2,1,0:T(8,128)(2,1)} %param.15) | copy-start | bytes 3145732
  356.9 47.5 %copy-start.30 = (u32[32]{0:T(128)S(1)}, u32[32]{0:T(128)}, u32[]{:S(2)}) copy-start(u32[32]{0:T(128)} %constant.63) | copy-start | bytes 388
  356.9 271.7 %all-reduce.9.cloned.1.call-start = ((), (), s32[]{:S(2)}) async-start(), calls=%async_computation.13 | async-start | bytes 516096
  402.9 0.7 copy-start.23
  403.6 303.7 %reduce-scatter.7.cloned.1.call-start = ((), (), s32[]{:S(2)}) async-start(), calls=%async_computation.7 | async-start | bytes 5242880 | tf_op jit(solution)/shard_map/reduce_scatter | solution.py:1027
  404.4 340.3 %all-reduce.11.cloned.1.call-start = ((), (), s32[]{:S(2)}) async-start(), calls=%async_computation.14 | async-start | bytes 262144
  457.8 249.5 %copy-start.20 = (bf16[1024,512]{1,0:T(8,128)(2,1)S(1)}, bf16[1024,512]{1,0:T(8,128)(2,1)}, u32[]{:S(2)}) copy-start(bf16[1024,512]{1,0:T(8,128)(2,1)} %reduce-scatter.9.cloned.1.call-done) | copy-start | bytes 3145732
  457.8 249.5 %copy-start.22 = (bf16[2,1,512,512]{3,2,1,0:T(8,128)(2,1)S(1)}, bf16[2,1,512,512]{3,2,1,0:T(8,128)(2,1)}, u32[]{:S(2)}) copy-start(bf16[2,1,512,512]{3,2,1,0:T(8,128)(2,1)} %param.16) | copy-start | bytes 3145732
  630.4 0.7 copy-start.25
  631.1 135.7 %reduce-scatter.15.cloned.1.call-start = ((), (), s32[]{:S(2)}) async-start(), calls=%async_computation.11 | async-start | bytes 327680 | tf_op jit(solution)/shard_map/reduce_scatter | solution.py:1057
Sparse Core Ops, SparseCore 0:
  18.9 28.7 all-gather.5
  324.0 75.9 reduce-scatter.8
  403.8 51.8 reduce-scatter.16
  458.9 51.2 reduce-scatter.10
  514.0 57.2 reduce-scatter.12
  575.1 53.4 all-reduce.8
  630.9 76.3 reduce-scatter.6
  709.7 34.9 all-reduce.10
  747.5 19.2 reduce-scatter.14
